TPU v7x, 256 devices: a whole 4x4x8 slice. The times are simulated.
256 devices in a mesh: leaf: 32 (over z_lo, x, core), head: 8 (over z_hi, y).
Axes of the slice: x: 4, y: 4, z: 8 (z_hi: 2, z_lo: 4; z = z_hi * 4 + z_lo), core: 2. Of those that a mesh axis runs over, the one named last changes fastest.
Arguments:
- queries: bfloat16 [6144, 73728], P('leaf', 'head'), may hold values from -80 to 80
- d_out: bfloat16 [6144, 65536], P('leaf', 'head'), may hold values from -24 to 24
- branch_latent: bfloat16 [6144, 576], P('leaf'), may hold values from -6 to 6
- trunk_latent: bfloat16 [512, 8, 576], P('leaf'), may hold values from -6 to 6
- ancestors: int32 [32, 32], replicated, may hold values from 0 to 511, as said below
- anc_count: int32 [32], replicated, may hold values from 24 to 32, as said below
Outputs:
- d_queries: bfloat16 [6144, 73728], P('leaf', 'head')
- d_branch: float32 [6144, 576], P(('leaf', 'head'))
- d_trunk: float32 [512, 8, 576], P('leaf', 'head')
Inputs may be any that keep to these rules, and one draw needn't show every extreme that they name: `ancestors`: each row lists 32 different trunk blocks; the owner of a block is its number // 16; a row lists 2 blocks of each owner that it names, never more. `anc_count`: some branch has all 32 slots live.
All inputs are finite; a program needn't handle non-finite values.
Results may differ from a plain program's by a relative error of at most 0.014.
Values may be sent and summed in bfloat16 or wider, within the bound.
A program may use at most 128 MiB of HBM per device.

v0:
```python
import jax
import jax.numpy as jnp
from jax import lax
from jax.sharding import PartitionSpec as P

RANK = 512
QK_HEAD = 192
LATENT = 576
BLK = 8
ANC = 32


def local(queries, d_out, branch_latent, trunk_latent, ancestors, anc_count):
    tok_rows = queries.shape[0]
    heads_here = queries.shape[1] // LATENT
    leaf_count = lax.axis_size("leaf")
    own_index = lax.axis_index("leaf")
    trunk_count = trunk_latent.shape[0]
    far_rows = ANC * BLK
    score_scale = float(QK_HEAD) ** (-0.5)
    positions = jnp.arange(ANC, dtype=jnp.int32)
    own_ancestors = lax.dynamic_index_in_dim(ancestors, own_index, 0, keepdims=False)
    own_count = lax.dynamic_index_in_dim(anc_count, own_index, 0, keepdims=False)
    valid_mine = positions < own_count
    everything = lax.all_gather(trunk_latent, "leaf", axis=0, tiled=True)
    far_data = jnp.take(everything, own_ancestors, axis=0)
    key_rows = jnp.concatenate([far_data.reshape(far_rows, LATENT), branch_latent], axis=0)
    far_ok = jnp.arange(far_rows, dtype=jnp.int32) // BLK < own_count
    causal = (
        jnp.arange(tok_rows, dtype=jnp.int32)[None, :]
        <= jnp.arange(tok_rows, dtype=jnp.int32)[:, None]
    )
    allowed = jnp.concatenate(
        [jnp.broadcast_to(far_ok[None, :], (tok_rows, far_rows)), causal], axis=1
    )
    query_heads = queries.reshape(tok_rows, heads_here, LATENT)
    grad_heads = d_out.reshape(tok_rows, heads_here, RANK)
    scores = (
        jnp.einsum("thc,kc->htk", query_heads, key_rows, preferred_element_type=jnp.float32)
        * score_scale
    )
    scores = jnp.where(allowed[None], scores, -1e30)
    row_max = jnp.max(scores, axis=2, keepdims=True)
    expo = jnp.exp(scores - row_max)
    attn = expo / jnp.sum(expo, axis=2, keepdims=True)
    attn_low = attn.astype(jnp.bfloat16)
    d_prob = jnp.einsum(
        "thr,kr->htk", grad_heads, key_rows[:, :RANK], preferred_element_type=jnp.float32
    )
    row_delta = jnp.sum(attn * d_prob, axis=2, keepdims=True)
    d_score = (attn * (d_prob - row_delta)).astype(jnp.bfloat16)
    d_query = (
        jnp.einsum("htk,kc->thc", d_score, key_rows, preferred_element_type=jnp.float32)
        * score_scale
    )
    d_queries = d_query.astype(jnp.bfloat16).reshape(tok_rows, heads_here * LATENT)
    d_key = (
        jnp.einsum("htk,thc->kc", d_score, query_heads, preferred_element_type=jnp.float32)
        * score_scale
    )
    d_value = jnp.einsum("htk,thr->kr", attn_low, grad_heads, preferred_element_type=jnp.float32)
    d_key = d_key + jnp.pad(d_value, ((0, 0), (0, LATENT - RANK)))
    d_branch = lax.psum_scatter(d_key[far_rows:], "head", scatter_dimension=0, tiled=True)
    far_grad = d_key[:far_rows].reshape(ANC, BLK, LATENT)
    far_grad = jnp.where(valid_mine[:, None, None], far_grad, 0.0)
    grad_rows = far_grad.shape[1]
    spread = (
        jnp.zeros((trunk_count * leaf_count, grad_rows, LATENT), jnp.float32)
        .at[own_ancestors]
        .add(far_grad)
    )
    owned_sum = lax.psum_scatter(
        spread.astype(jnp.bfloat16), "leaf", scatter_dimension=0, tiled=True
    )
    d_trunk = lax.psum_scatter(owned_sum, "head", scatter_dimension=1, tiled=True).astype(
        jnp.float32
    )
    return (d_queries, d_branch, d_trunk)


def solution(mesh):
    return jax.shard_map(
        local,
        mesh=mesh,
        in_specs=(
            P("leaf", "head"),
            P("leaf", "head"),
            P("leaf", None),
            P("leaf", None, None),
            P(),
            P(),
        ),
        out_specs=(P("leaf", "head"), P(("leaf", "head"), None), P("leaf", "head", None)),
        check_vma=False,
    )
```

profile of v0, /device:TPU:6, one launch (start us, length us, event | category | flops | bytes accessed | tf_op | source)
XLA Modules:
  0.0 435.4 jit_solution(4776977271193443856)
XLA Ops:
  7.2 0.0 all-gather.2.cloned.1.call-start
  7.2 0.7 all-gather.2.cloned.1.call-update
  7.9 0.0 reduce-scatter.6.cloned.1.call-start
  7.9 1.2 dynamic_slice.9
  9.2 0.7 compare_and_fusion
  9.9 0.1 broadcast_in_dim.55
  10.0 0.1 broadcast_in_dim.56
  10.1 0.0 copy-start.3
  10.1 7.0 %reshape.77 = bf16[192,16,576]{2,1,0:T(8,128)(2,1)} reshape(bf16[192,9216]{1,0:T(8,128)(2,1)} %param.6) | data formatting | bytes 7077888 | tf_op jit(solution)/shard_map/reshape | solution.py:36
  17.1 0.7 fusion.41
  17.8 0.7 fusion.42
  18.5 0.6 iota_compare_fusion.1
  19.2 56.7 %all-gather.2.cloned.1.call-done = bf16[512,8,576]{2,1,0:T(8,128)(2,1)} async-done(((bf16[16,8,576]{2,1,0:T(8,128)(2,1)}), bf16[512,8,576]{2,1,0:T(8,128)(2,1)}) %all-gather.2.cloned.1.call-update) | async-done | bytes 4718608 | tf_op jit(solution)/shard_map/all_gather | solution.py:25
  75.9 3.1 gather_fusion
  79.0 0.1 bitcast_select_fusion.4
  79.1 0.0 copy-done.3
  79.1 4.8 %fusion.8 = f32[448,192,16]{0,1,2:T(8,128)S(1)} fusion(bf16[192,16,576]{2,1,0:T(8,128)(2,1)} %reshape.77, bf16[192,576]{1,0:T(8,128)(2,1)S(1)} %copy-done.3, bf16[256,576]{1,0:T(8,128)(2,1)S(1)} %bitcast_select_fusion.4), kind=kOutput, calls=%fused_computation.15 | convolution fusion | flops 1586479104 | bytes 9560064 | tf_op jit(solution)/shard_map/thc,kc->htk/dot_general | solution.py:39
  83.9 0.0 copy-start.2
  83.9 3.4 fusion.48
  87.3 0.0 copy-done.2
  87.4 2.3 fusion.26
  89.7 2.7 fusion.1
  92.4 0.0 copy-start
  92.4 1.2 fusion.3
  93.6 0.9 copy-done
  94.5 2.5 fusion.31
  97.0 0.0 copy-start.1
  97.0 1.0 copy-done.1
  98.0 1.0 fusion.34
  99.0 4.7 %broadcast_in_dim.62 = f32[512,8,576]{2,1,0:T(8,128)} broadcast(f32[]{:T(128)} %constant.62.clone.1), dimensions={} | broadcast | bytes 9437188 | tf_op jit(solution)/shard_map/broadcast_in_dim | solution.py:68
  103.6 5.0 %scatter_fusion = f32[512,8,576]{2,1,0:T(8,128)} fusion(f32[512,8,576]{2,1,0:T(8,128)} %broadcast_in_dim.62, s32[32]{0:T(128)S(1)} %fusion.42, f32[32,8,576]{2,1,0:T(8,128)} %fusion.34), kind=kCustom, calls=%fused_computation.1 | custom fusion | flops 147456 | bytes 1769600 | tf_op jit(solution)/shard_map/scatter-add | solution.py:70
  108.6 6.9 %convert_element_type.24 = bf16[512,8,576]{2,1,0:T(8,128)(2,1)} convert(f32[512,8,576]{2,1,0:T(8,128)} %scatter_fusion) | non-fusion elementwise | flops 2359296 | bytes 14155776 | tf_op jit(solution)/shard_map/convert_element_type | solution.py:73
  115.5 0.0 reduce-scatter.6.cloned.1.call-update
  115.5 0.0 reduce-scatter.8.cloned.1.call-start
  115.5 136.9 %reduce-scatter.6.cloned.1.call-done = bf16[16,8,576]{2,1,0:T(8,128)(2,1)} async-done(((bf16[512,8,576]{2,1,0:T(8,128)(2,1)}), bf16[16,8,576]{2,1,0:T(8,128)(2,1)}) %reduce-scatter.6.cloned.1.call-update) | async-done | bytes 147472 | tf_op jit(solution)/shard_map/reduce_scatter | solution.py:72
  252.4 1.6 copy.23
  254.0 0.0 reduce-scatter.8.cloned.1.call-update
  254.0 0.0 reduce-scatter.10.cloned.1.call-start
  254.1 1.8 slice.16
  255.9 0.0 reduce-scatter.10.cloned.1.call-update
  255.9 3.8 fusion.5
  259.7 4.2 copy.20
  263.9 7.0 %reshape.79 = bf16[192,9216]{1,0:T(8,128)(2,1)} reshape(bf16[192,16,576]{2,1,0:T(8,128)(2,1)} %copy.20) | data formatting | bytes 7077888 | tf_op jit(solution)/shard_map/reshape | solution.py:56
  270.9 75.0 %reduce-scatter.8.cloned.1.call-done = bf16[16,1,576]{2,0,1:T(8,128)(2,1)} async-done(((bf16[16,8,576]{2,0,1:T(8,128)(2,1)}), bf16[16,1,576]{2,0,1:T(8,128)(2,1)}) %reduce-scatter.8.cloned.1.call-update) | async-done | bytes 18448 | tf_op jit(solution)/shard_map/reduce_scatter | solution.py:75
  345.8 1.4 copy.24
  347.2 81.6 %reduce-scatter.10.cloned.1.call-done = f32[24,576]{1,0:T(8,128)} async-done(((f32[192,576]{1,0:T(8,128)}), f32[24,576]{1,0:T(8,128)}) %reduce-scatter.10.cloned.1.call-update) | async-done | bytes 55312
  (4 shorter events, 0.1 us)
Async XLA Ops:
  7.2 68.7 %all-gather.2.cloned.1.call-start = ((), (), s32[]{:S(2)}) async-start(), calls=%async_computation.3 | async-start | bytes 5406720 | tf_op jit(solution)/shard_map/all_gather | solution.py:25
  7.9 244.5 %reduce-scatter.6.cloned.1.call-start = ((), (), s32[]{:S(2)}) async-start(), calls=%async_computation.4 | async-start | bytes 5406720 | tf_op jit(solution)/shard_map/reduce_scatter | solution.py:72
  10.1 69.0 %copy-start.3 = (bf16[192,576]{1,0:T(8,128)(2,1)S(1)}, bf16[192,576]{1,0:T(8,128)(2,1)}, u32[]{:S(2)}) copy-start(bf16[192,576]{1,0:T(8,128)(2,1)} %param.8) | copy-start | bytes 663556
  83.9 3.4 copy-start.2
  92.4 2.1 copy-start
  97.0 1.0 copy-start.1
  115.5 230.3 %reduce-scatter.8.cloned.1.call-start = ((), (), s32[]{:S(2)}) async-start(), calls=%async_computation.5 | async-start | bytes 184320 | tf_op jit(solution)/shard_map/reduce_scatter | solution.py:75
  254.0 174.8 %reduce-scatter.10.cloned.1.call-start = ((), (), s32[]{:S(2)}) async-start(), calls=%async_computation.6 | async-start | bytes 552960
Sparse Core Ops, SparseCore 0:
  9.8 66.0 all-gather.1
  115.6 136.7 reduce-scatter.5
  256.1 89.7 reduce-scatter.7
  350.1 78.6 reduce-scatter.9
where the time goes:
time: 436 us; the launch traced here: 435 us
  waiting for transfers between devices  351 us (81%)
  local copies, waits for them, and re-layouts  34.1 us (8%)
  other arithmetic  20.3 us (5%)
  matrix products  16.1 us (4%)
  between operations  13.9 us (3%)
    reduce_scatter x1, waiting for transfers between devices, local(): lax.psum_scatter(spread.astype(jnp.bfloat16), 'leaf', scatter_dimension=0...  137 us
    unnamed x5, waiting for transfers between devices  82.3 us
    reduce_scatter x1, waiting for transfers between devices, local(): lax.psum_scatter(owned_sum, 'head', scatter_dimension=1, tiled=True)  75 us
    all_gather x1, waiting for transfers between devices, local(): everything = lax.all_gather(trunk_latent, 'leaf', axis=0, tiled=True)  56.7 us
  transfers between devices with their start and end apart: 4, of which 4 were waited for; matrix products, arithmetic and copies ran while one was open for 7% of the time, Pallas kernels for 0%

commit v1 on v0

v1 whole, which is shorter than its diff:
```python
import functools

import jax
import jax.numpy as jnp
from jax import lax
from jax.experimental import pallas as pl
from jax.experimental.pallas import tpu as pltpu
from jax.sharding import PartitionSpec as P

F32, BF16 = jnp.float32, jnp.bfloat16
SCALE = float(192) ** -0.5
LOG2E = 1.4426950408889634
LEAF = 32
WIDE = 640


def dot(a, b, ca, cb):
    return lax.dot_general(a, b, (((ca,), (cb,)), ((), ())), preferred_element_type=F32)


def iota(shape, dim):
    return lax.broadcasted_iota(jnp.int32, shape, dim)


def listed_block(anc, leaf, branch, pick):
    rows = branch.shape[0]
    expand = (branch == iota((rows, LEAF), 1)).astype(F32).astype(BF16)
    owner = dot(expand, (anc >> 4).astype(F32).astype(BF16), 1, 0)
    local = dot(expand, (anc & 15).astype(F32).astype(BF16), 1, 0)
    mine = jnp.where(owner == leaf.astype(F32), 1.0, 0.0)
    before = jnp.where(iota((LEAF, LEAF), 0) < iota((LEAF, LEAF), 1), 1.0, 0.0).astype(BF16)
    rank = dot(mine.astype(BF16), before, 1, 0)
    chosen = jnp.where(rank == pick.astype(F32), mine, 0.0)
    return jnp.sum(chosen * (local + 1.0), axis=1, keepdims=True)


def owner_and_rank(row, slot):
    rows = slot.shape[0]
    owners = (row >> 4).astype(F32)
    at = iota((rows, LEAF), 1)
    owner = jnp.sum(jnp.where(at == slot, owners, 0.0), axis=1, keepdims=True)
    rank = jnp.sum(jnp.where((owners == owner) & (at < slot), 1.0, 0.0), axis=1, keepdims=True)
    return owner, rank


def remote(src, dst, send, recv, where):
    return pltpu.make_async_remote_copy(
        src_ref=src, dst_ref=dst, send_sem=send, recv_sem=recv, device_id=where, device_id_type=pl.DeviceIdType.MESH
    )


def signal(sem, where):
    pl.semaphore_signal(sem, inc=1, device_id=where, device_id_type=pl.DeviceIdType.MESH)


def gather(anc_ref, trunk_ref, keys_ref, out, got, tall, slabs, out_send, out_recv, ring_send, ring_recv):
    leaf, head = lax.axis_index("leaf"), lax.axis_index("head")
    deep, y = head // 4, lax.rem(head, 4)
    right = {"head": deep * 4 + lax.rem(y + 1, 4)}
    left = {"head": deep * 4 + lax.rem(y + 3, 4)}
    barrier = pltpu.get_barrier_semaphore()

    def greet(k, c):
        signal(barrier, {"leaf": lax.rem(leaf + k, LEAF)})
        return c

    lax.fori_loop(1, LEAF, greet, 0)
    signal(barrier, left)
    signal(barrier, right)

    i = iota((128, 1), 0)
    block = listed_block(anc_ref[...], leaf, i // 4, (i // 2) % 2)
    want = (block - 1.0) * 8.0 + (i % 2 + 2 * y).astype(F32)
    pick = jnp.where(want == iota((128, 128), 1).astype(F32), 1.0, 0.0).astype(BF16)
    trunk = trunk_ref[...].astype(F32).reshape(128, 576).astype(BF16)
    rows = dot(pick, jnp.concatenate([trunk, jnp.zeros((128, WIDE - 576), BF16)], axis=1), 1, 0)
    for b in range(LEAF):
        out[b] = rows[4 * b:4 * b + 4].astype(BF16)

    pl.semaphore_wait(barrier, LEAF + 1)

    def send(k, c):
        to = lax.rem(leaf + k, LEAF)
        remote(out.at[to], got.at[leaf], out_send.at[k], out_recv.at[leaf], {"leaf": to}).start()
        return c

    lax.fori_loop(1, LEAF, send, 0)
    mine = pltpu.make_async_copy(out.at[leaf], got.at[leaf], out_recv.at[leaf])
    mine.start()

    i = iota((64, 1), 0)
    owner, rank = owner_and_rank(anc_ref[pl.ds(leaf, 1), :], i % 32)
    want = owner * 4.0 + rank * 2.0 + (i // 32).astype(F32)
    pick = jnp.where(want == iota((64, 128), 1).astype(F32), 1.0, 0.0).astype(BF16)

    mine.wait()

    def receive(k, c):
        source = lax.rem(leaf + k, LEAF)
        remote(out.at[source], got.at[source], out_send.at[k], out_recv.at[source], {"leaf": source}).wait()
        return c

    lax.fori_loop(1, LEAF, receive, 0)
    for b in range(LEAF):
        tall[4 * b:4 * b + 4, :] = got[b].astype(F32)
    slabs[y] = dot(pick, tall[...].astype(BF16), 1, 0).astype(BF16)

    def hop(k, slab, half, where):
        part = slabs.at[slab, pl.ds(32 * half, 32)]
        return remote(part, part, ring_send.at[k], ring_recv.at[k], where)

    up, down = lax.rem(y + 3, 4), lax.rem(y + 1, 4)
    first = [hop(0, y, 0, right), hop(1, y, 1, left), hop(2, y, 1, right), hop(3, y, 0, left)]
    for copy in first:
        copy.start()
    hop(0, up, 0, right).wait_recv()
    pass_right = hop(4, up, 0, right)
    pass_right.start()
    hop(1, down, 1, left).wait_recv()
    pass_left = hop(5, down, 1, left)
    pass_left.start()
    far = lax.rem(y + 2, 4)
    hop(2, up, 1, right).wait_recv()
    hop(3, down, 0, left).wait_recv()
    hop(4, far, 0, right).wait_recv()
    hop(5, far, 1, left).wait_recv()
    for copy in first + [pass_right, pass_left]:
        copy.wait_send()
    for s in range(4):
        keys_ref[64 * s:64 * s + 64, :] = slabs[s]


def gather_call(ancestors, trunk):
    return pl.pallas_call(
        gather,
        out_shape=jax.ShapeDtypeStruct((256, WIDE), BF16),
        in_specs=[pl.BlockSpec(memory_space=pltpu.VMEM)] * 2,
        out_specs=pl.BlockSpec(memory_space=pltpu.VMEM),
        scratch_shapes=[
            pltpu.VMEM((LEAF, 4, WIDE), BF16),
            pltpu.VMEM((LEAF, 4, WIDE), BF16),
            pltpu.VMEM((128, WIDE), F32),
            pltpu.VMEM((4, 64, WIDE), BF16),
            pltpu.SemaphoreType.DMA((LEAF,)),
            pltpu.SemaphoreType.DMA((LEAF,)),
            pltpu.SemaphoreType.DMA((6,)),
            pltpu.SemaphoreType.DMA((6,)),
        ],
        compiler_params=pltpu.CompilerParams(collective_id=0, has_side_effects=True),
        name="gather",
    )(ancestors, trunk)


def attend(G, count_ref, far_ref, own_ref, q_ref, do_ref, dq_ref, dk_ref, ke, ko, bias, acc_e, acc_o, acc_v):
    step = pl.program_id(0)
    T = 192 * G
    @pl.when(step == 0)
    def _():
        ke[0:256, :] = far_ref[...]
        ke[256:448, :] = jnp.concatenate([own_ref[...], jnp.zeros((192, 64), BF16)], axis=1)
        ko[...] = pltpu.roll(ke[...].astype(F32), 64, 1).astype(BF16)
        row = lax.broadcasted_iota(jnp.int32, (256, 192), 0)
        bias[0:256, :] = jnp.where(row % 32 < count_ref[lax.axis_index("leaf")], 0.0, -1e30)
        row = lax.broadcasted_iota(jnp.int32, (192, 192), 0)
        col = lax.broadcasted_iota(jnp.int32, (192, 192), 1)
        bias[256:448, :] = jnp.where(row <= col, 0.0, -1e30)
        acc_e[...] = jnp.zeros_like(acc_e)
        acc_o[...] = jnp.zeros_like(acc_o)
        acc_v[...] = jnp.zeros_like(acc_v)
    for par in range(2):
        K = (ke, ko)[par][...]
        Q = jnp.concatenate([q_ref[:, 1152 * g + 512 * par:1152 * g + 512 * par + 640] for g in range(G)], axis=0)
        DO = jnp.concatenate([do_ref[:, 1024 * g + 512 * par:1024 * g + 512 * par + 512] for g in range(G)], axis=0)
        s = dot(K, Q, 1, 1)
        dp = dot(ke[:, 0:512], DO, 1, 1)
        b = bias[...]
        s = s + jnp.concatenate([b] * G, axis=1)
        m = jnp.max(s, axis=0, keepdims=True)
        e = jnp.exp2((s - m) * (SCALE * LOG2E))
        p = e * (1.0 / jnp.sum(e, axis=0, keepdims=True))
        delta = jnp.sum(p * dp, axis=0, keepdims=True)
        ds = (p * (dp - delta)).astype(BF16)
        acc_v[...] += dot(p.astype(BF16), DO, 1, 0)
        acc = (acc_e, acc_o)[par]
        acc[...] += dot(ds, Q, 1, 0)
        dq = dot(ds, K, 0, 0) * SCALE
        if par == 0:
            dqe = dq
        else:
            for g in range(G):
                r = slice(192 * g, 192 * g + 192)
                c = 1152 * g
                dq_ref[:, c:c + 512] = dqe[r, 0:512].astype(BF16)
                dq_ref[:, c + 512:c + 640] = (dqe[r, 512:640] + dq[r, 0:128]).astype(BF16)
                dq_ref[:, c + 640:c + 1152] = dq[r, 128:640].astype(BF16)
    @pl.when(step == pl.num_programs(0) - 1)
    def _():
        dk = (acc_e[...] + pltpu.roll(acc_o[...], 576, 1)) * SCALE
        acc_e[:, 0:512] = dk[:, 0:512] + acc_v[...]
        acc_e[:, 512:640] = dk[:, 512:640]
        for h in range(8):
            dk_ref[h, 0:32, :] = acc_e[32 * h:32 * h + 32, :].astype(BF16)
            dk_ref[h, 32:56, :] = acc_e[256 + 24 * h:280 + 24 * h, :].astype(BF16)


def attend_call(G, count, far, own, q, do):
    return pl.pallas_call(
        functools.partial(attend, G),
        grid=(8 // G,),
        out_shape=(jax.ShapeDtypeStruct((192, 9216), BF16), jax.ShapeDtypeStruct((8, 56, 640), BF16)),
        in_specs=[pl.BlockSpec(memory_space=pltpu.SMEM),
                  pl.BlockSpec((256, 640), lambda i: (0, 0)), pl.BlockSpec((192, 576), lambda i: (0, 0)),
                  pl.BlockSpec((192, 1152 * G), lambda i: (0, i)), pl.BlockSpec((192, 1024 * G), lambda i: (0, i))],
        out_specs=(pl.BlockSpec((192, 1152 * G), lambda i: (0, i)), pl.BlockSpec((8, 56, 640), lambda i: (0, 0, 0))),
        scratch_shapes=[pltpu.VMEM((448, 640), BF16)] * 2 + [pltpu.VMEM((448, 192), F32)]
        + [pltpu.VMEM((448, 640), F32)] * 2 + [pltpu.VMEM((448, 512), F32)],
        name="attend",
    )(count, far, own, q, do)


def reduce(anc_ref, dk_ref, branch_ref, trunk_ref, near, pair, pair_in, out, got, tall,
           near_send, near_recv, pair_send, pair_recv, out_send, out_recv):
    leaf, head = lax.axis_index("leaf"), lax.axis_index("head")
    deep, y = head // 4, lax.rem(head, 4)
    me = deep * LEAF + leaf
    barrier = pltpu.get_barrier_semaphore()

    def plane(p):
        return {"leaf": lax.rem(p, LEAF), "head": (p // LEAF) * 4 + y}

    def greet(k, c):
        signal(barrier, plane(lax.rem(me + k, 2 * LEAF)))
        return c

    lax.fori_loop(1, 2 * LEAF, greet, 0)
    for k in range(1, 4):
        signal(barrier, {"head": deep * 4 + lax.rem(y + k, 4)})

    i = iota((64, 1), 0)
    owner, rank = owner_and_rank(anc_ref[pl.ds(leaf, 1), :], i % 32)
    want = (i // 32).astype(F32) * 64.0 + owner * 2.0 + rank
    spread = jnp.where(want == iota((64, 128), 1).astype(F32), 1.0, 0.0).astype(BF16)
    i = iota((128, 1), 0)
    block = listed_block(anc_ref[...], leaf, (i // 2) % 32, i % 2)
    collect = jnp.where(block - 1.0 == iota((128, 16), 1).astype(F32), 1.0, 0.0).astype(BF16)

    pl.semaphore_wait(barrier, 2 * LEAF + 2)

    def sent(part, rows, k, half):
        to = lax.rem(y + k, 4)
        n = part * 8 + half * 4 + k
        return remote(dk_ref.at[half * 4 + to, rows], near.at[k, half, rows], near_send.at[n], near_recv.at[n],
                      {"head": deep * 4 + to})

    parts = (pl.ds(0, 32), pl.ds(32, 24))
    copies = [[sent(part, parts[part], k, half) for k in (2, 1, 3) for half in range(2)] for part in range(2)]
    for copy in copies[0] + copies[1]:
        copy.start()
    for copy in copies[0]:
        copy.wait_recv()
    sums = []
    for half in range(2):
        total = dk_ref[half * 4 + y, 0:32, :].astype(F32)
        for k in range(1, 4):
            total = total + near[k, half, 0:32, :].astype(F32)
        sums.append(total.astype(BF16))
    rows = dot(spread, jnp.concatenate(sums, axis=0), 0, 0)
    for d in range(2 * LEAF):
        out[d] = rows[2 * d:2 * d + 2].astype(BF16)

    def send(k, c):
        to = lax.rem(me + k, 2 * LEAF)
        remote(out.at[to], got.at[me], out_send.at[k], out_recv.at[me], plane(to)).start()
        return c

    lax.fori_loop(1, 2 * LEAF, send, 0)
    mine = pltpu.make_async_copy(out.at[me], got.at[me], out_recv.at[me])
    mine.start()

    for copy in copies[1]:
        copy.wait_recv()
    for half in range(2):
        total = dk_ref[half * 4 + y, 32:56, :].astype(F32)
        for k in range(1, 4):
            total = total + near[k, half, 32:56, :].astype(F32)
        pair[half] = total
    pair_out = remote(pair.at[1 - deep], pair_in, pair_send, pair_recv, {"head": (1 - deep) * 4 + y})
    pair_out.start()

    mine.wait()

    def receive(k, c):
        source = lax.rem(me + k, 2 * LEAF)
        remote(out.at[source], got.at[source], out_send.at[k], out_recv.at[source], plane(source)).wait()
        return c

    lax.fori_loop(1, 2 * LEAF, receive, 0)
    for d in range(2 * LEAF):
        tall[2 * d:2 * d + 2, :] = got[d].astype(F32)
    trunk_ref[...] = dot(collect, tall[...].astype(BF16), 0, 0)[:, 0:576]
    pair_out.wait()
    branch_ref[...] = (pair[deep] + pair_in[...])[:, 0:576]
    for copy in copies[0] + copies[1]:
        copy.wait_send()


def reduce_call(ancestors, dk):
    return pl.pallas_call(
        reduce,
        out_shape=(jax.ShapeDtypeStruct((24, 576), F32), jax.ShapeDtypeStruct((16, 576), F32)),
        in_specs=[pl.BlockSpec(memory_space=pltpu.VMEM)] * 2,
        out_specs=(pl.BlockSpec(memory_space=pltpu.VMEM),) * 2,
        scratch_shapes=[
            pltpu.VMEM((4, 2, 56, WIDE), BF16),
            pltpu.VMEM((2, 24, WIDE), F32),
            pltpu.VMEM((24, WIDE), F32),
            pltpu.VMEM((2 * LEAF, 2, WIDE), BF16),
            pltpu.VMEM((2 * LEAF, 2, WIDE), BF16),
            pltpu.VMEM((128, WIDE), F32),
            pltpu.SemaphoreType.DMA((16,)),
            pltpu.SemaphoreType.DMA((16,)),
            pltpu.SemaphoreType.DMA,
            pltpu.SemaphoreType.DMA,
            pltpu.SemaphoreType.DMA((2 * LEAF,)),
            pltpu.SemaphoreType.DMA((2 * LEAF,)),
        ],
        compiler_params=pltpu.CompilerParams(collective_id=1, has_side_effects=True),
        name="reduce",
    )(ancestors, dk)


def local(queries, d_out, branch_latent, trunk_latent, ancestors, anc_count):
    far = gather_call(ancestors, trunk_latent)
    d_queries, dk = attend_call(4, anc_count, far, branch_latent, queries, d_out)
    d_branch, d_trunk = reduce_call(ancestors, dk)
    return d_queries, d_branch, d_trunk[:, None, :]


def solution(mesh):
    return jax.shard_map(
        local,
        mesh=mesh,
        in_specs=(P("leaf", "head"), P("leaf", "head"), P("leaf", None), P("leaf", None, None), P(), P()),
        out_specs=(P("leaf", "head"), P(("leaf", "head"), None), P("leaf", "head", None)),
        check_vma=False,
    )
```

time: 436 us -> 69.7 us (0.16)
  the two profiles are of different devices: /device:TPU:6 before, /device:TPU:1 now
where the time goes in v1:
time: 69.7 us; the launch traced here: 69.4 us
  Pallas kernels  65.9 us (95%)
  local copies, waits for them, and re-layouts  2.89 us (4%)
    pallas_call x1, Pallas kernels, reduce_call(): pl.pallas_call(reduce, out_shape=(jax.ShapeDtypeStruct((24, 576), F32), j...  28.5 us
    pallas_call x1, Pallas kernels, gather_call(): pl.pallas_call(gather, out_shape=jax.ShapeDtypeStruct((256, WIDE), BF16),...  20.9 us
    pallas_call x1, Pallas kernels, attend_call(): pl.pallas_call(functools.partial(attend, G), grid=(8 // G,), out_shape=(j...  16.5 us
    unnamed x2, local copies, waits for them, and re-layouts  2.89 us

profile of v1, /device:TPU:1, one launch (start us, length us, event | category | flops | bytes accessed | tf_op | source)
XLA Modules:
  0.0 69.4 jit_solution(17508825133778596809)
XLA Ops:
  0.6 20.9 %gather.1.far_ref = bf16[256,640]{1,0:T(8,128)(2,1)} custom-call(s32[32,32]{1,0:T(8,128)} %anc_ref.3, bf16[16,8,576]{2,1,0:T(8,128)(2,1)} %trunk_ref.1), custom_call_target="tpu_custom_call" | custom-call | tf_op jit(solution)/shard_map/gather/pallas_call | solution.py:134
  21.5 16.5 %attend.1 = (bf16[192,9216]{1,0:T(8,128)(2,1)}, bf16[8,56,640]{2,1,0:T(8,128)(2,1)}) custom-call(s32[32]{0:T(128)} %count_ref.1, bf16[256,640]{1,0:T(8,128)(2,1)} %gather.1.far_ref, bf16[192,576]{1,0:T(8,128)(2,1)} %own_ref.1, bf16[192,9216]{1,0:T(8,128)(2,1)} %q_ref.1, bf16[192,8192]{1,0:T(8,128)(2,1)} %do_ref.1), custom_call_target="tpu_custom_call" | custom-call | tf_op jit(solution)/shard_map/attend/pallas_call | solution.py:207
  38.1 28.5 %reduce.1 = (f32[24,576]{1,0:T(8,128)}, f32[16,576]{1,0:T(8,128)}) custom-call(s32[32,32]{1,0:T(8,128)} %anc_ref.3, bf16[8,56,640]{2,1,0:T(8,128)(2,1)} %get-tuple-element.8.dk_ref), custom_call_target="tpu_custom_call" | custom-call | tf_op jit(solution)/shard_map/reduce/pallas_call | solution.py:308
  66.5 1.4 %copy.9 = f32[16,1,576]{2,1,0:T(1,128)} copy(f32[16,1,576]{2,0,1:T(8,128)} %bitcast.1) | data formatting | bytes 73728
  68.0 1.5 %copy.11 = f32[24,576]{1,0:T(8,128)} copy(f32[24,576]{1,0:T(8,128)} %get-tuple-element.18) | data formatting | bytes 110592

commit v2 on v0

v2 whole, which is shorter than its diff:
```python
import functools

import jax
import jax.numpy as jnp
from jax import lax
from jax.experimental import pallas as pl
from jax.experimental.pallas import tpu as pltpu
from jax.sharding import PartitionSpec as P

F32, BF16 = jnp.float32, jnp.bfloat16
SCALE = float(192) ** -0.5
LOG2E = 1.4426950408889634
LEAF = 32
WIDE = 640


def dot(a, b, ca, cb):
    return lax.dot_general(a, b, (((ca,), (cb,)), ((), ())), preferred_element_type=F32)


def iota(shape, dim):
    return lax.broadcasted_iota(jnp.int32, shape, dim)


def listed_block(anc, leaf, branch, pick):
    rows = branch.shape[0]
    expand = (branch == iota((rows, LEAF), 1)).astype(F32).astype(BF16)
    owner = dot(expand, (anc >> 4).astype(F32).astype(BF16), 1, 0)
    local = dot(expand, (anc & 15).astype(F32).astype(BF16), 1, 0)
    mine = jnp.where(owner == leaf.astype(F32), 1.0, 0.0)
    before = jnp.where(iota((LEAF, LEAF), 0) < iota((LEAF, LEAF), 1), 1.0, 0.0).astype(BF16)
    rank = dot(mine.astype(BF16), before, 1, 0)
    chosen = jnp.where(rank == pick.astype(F32), mine, 0.0)
    return jnp.sum(chosen * (local + 1.0), axis=1, keepdims=True)


def owner_and_rank(row, slot):
    rows = slot.shape[0]
    owners = (row >> 4).astype(F32)
    at = iota((rows, LEAF), 1)
    owner = jnp.sum(jnp.where(at == slot, owners, 0.0), axis=1, keepdims=True)
    rank = jnp.sum(jnp.where((owners == owner) & (at < slot), 1.0, 0.0), axis=1, keepdims=True)
    return owner, rank


def remote(src, dst, send, recv, where):
    return pltpu.make_async_remote_copy(
        src_ref=src, dst_ref=dst, send_sem=send, recv_sem=recv, device_id=where, device_id_type=pl.DeviceIdType.MESH
    )


def signal(sem, where):
    pl.semaphore_signal(sem, inc=1, device_id=where, device_id_type=pl.DeviceIdType.MESH)


def fused(comm, anc_ref, cnt_ref, own_ref, trunk_ref, q_hbm, do_hbm, dq_hbm, branch_ref, spare_ref,
          qs, dos, keys, sown, dpown, p_own, ds, acc_k, acc_v, dq_out,
          g_out, g_got, g_tall, slabs, x_far, x_own, r_far, r_own, m_far, m_own, pair, pair_in, t_out, t_got, t_tall,
          load_sem, store_sem, g_send, g_recv, ring_send, ring_recv, far_send, far_recv, own_send, own_recv,
          pair_sem, t_send, t_recv):
    if comm:
        leaf, head = lax.axis_index("leaf"), lax.axis_index("head")
        deep, y = head // 4, lax.rem(head, 4)
        me = deep * LEAF + leaf
        right = {"head": deep * 4 + lax.rem(y + 1, 4)}
        left = {"head": deep * 4 + lax.rem(y + 3, 4)}

        def plane(p):
            return {"leaf": lax.rem(p, LEAF), "head": (p // LEAF) * 4 + y}

        barrier = pltpu.get_barrier_semaphore()

        def greet(k, c):
            signal(barrier, plane(lax.rem(me + k, 2 * LEAF)))
            return c

        lax.fori_loop(1, 2 * LEAF, greet, 0)
        signal(barrier, left)
        signal(barrier, right)
    else:
        leaf = 0

    loads = {}
    for u in range(2):
        for par in range(2):
            group = []
            for n in range(4):
                h = 4 * u + n
                at = pl.ds(192 * h, 192)
                k = 16 * u + 8 * par + 2 * n
                group.append(pltpu.make_async_copy(
                    q_hbm.at[:, pl.ds(1152 * h + 512 * par, WIDE)], qs.at[par, at], load_sem.at[k]))
                group.append(pltpu.make_async_copy(
                    do_hbm.at[:, pl.ds(1024 * h + 512 * par, 512)], dos.at[par, at], load_sem.at[k + 1]))
            for copy in group:
                copy.start()
            loads[u, par] = group
    chunks = [(u, par) for u in range(2) for par in range(2)]

    def q_of(u, par):
        return qs[par, 768 * u:768 * u + 768, :]

    def do_of(u, par):
        return dos[par, 768 * u:768 * u + 768, :]

    if comm:
        i = iota((128, 1), 0)
        block = listed_block(anc_ref[...], leaf, i // 4, (i // 2) % 2)
        want = (block - 1.0) * 8.0 + (4 * (i % 2) + y).astype(F32)
        pick = jnp.where(want == iota((128, 128), 1).astype(F32), 1.0, 0.0).astype(BF16)
        trunk = trunk_ref[...].astype(F32).reshape(128, 576).astype(BF16)
        rows = dot(pick, jnp.concatenate([trunk, jnp.zeros((128, WIDE - 576), BF16)], axis=1), 1, 0)
        for b in range(LEAF):
            g_out[b] = rows[4 * b:4 * b + 4].astype(BF16)
        i = iota((64, 1), 0)
        owner, rank = owner_and_rank(anc_ref[pl.ds(leaf, 1), :], i % 32)
        want = owner * 4.0 + rank * 2.0 + (i // 32).astype(F32)
        take = jnp.where(want == iota((64, 128), 1).astype(F32), 1.0, 0.0).astype(BF16)
        want = (i // 32).astype(F32) * 64.0 + owner * 2.0 + rank
        spread = jnp.where(want == iota((64, 128), 1).astype(F32), 1.0, 0.0).astype(BF16)
        i = iota((128, 1), 0)
        block = listed_block(anc_ref[...], leaf, (i // 2) % 32, i % 2)
        collect = jnp.where(block - 1.0 == iota((128, 16), 1).astype(F32), 1.0, 0.0).astype(BF16)

    own = own_ref[...]
    blank = jnp.zeros((192, 64), BF16)
    keys[0, 0:192, :] = jnp.concatenate([own, blank], axis=1)
    keys[1, 0:192, :] = pltpu.roll(jnp.concatenate([own, blank], axis=1).astype(F32), 64, 1).astype(BF16)
    causal = jnp.where(iota((192, 192), 0) <= iota((192, 192), 1), 0.0, -1e30)

    def own_scores(c):
        for copy in loads[chunks[c]]:
            copy.wait()
        u, par = chunks[c]
        s = dot(keys[par, 0:192, :], q_of(u, par), 1, 1)
        sown[c] = s + jnp.concatenate([causal] * 4, axis=1)
        dpown[c] = dot(keys[0, 0:192, 0:512], do_of(u, par), 1, 1)

    if comm:
        pl.semaphore_wait(barrier, 2 * LEAF + 1)

        def send(k, c):
            to = lax.rem(leaf + k, LEAF)
            remote(g_out.at[to], g_got.at[leaf], g_send.at[k], g_recv.at[leaf], {"leaf": to}).start()
            return c

        lax.fori_loop(1, LEAF, send, 0)
        mine = pltpu.make_async_copy(g_out.at[leaf], g_got.at[leaf], g_recv.at[leaf])
        mine.start()
        for c in range(4):
            own_scores(c)
        mine.wait()

        def receive(k, c):
            source = lax.rem(leaf + k, LEAF)
            remote(g_out.at[source], g_got.at[source], g_send.at[k], g_recv.at[source], {"leaf": source}).wait()
            return c

        lax.fori_loop(1, LEAF, receive, 0)
        for b in range(LEAF):
            g_tall[4 * b:4 * b + 4, :] = g_got[b].astype(F32)
        slabs[y] = dot(take, g_tall[...].astype(BF16), 1, 0).astype(BF16)

        def hop(k, slab, half, where):
            part = slabs.at[slab, pl.ds(32 * half, 32)]
            return remote(part, part, ring_send.at[k], ring_recv.at[k], where)

        up, down, far = lax.rem(y + 3, 4), lax.rem(y + 1, 4), lax.rem(y + 2, 4)
        ring = [hop(0, y, 0, right), hop(1, y, 1, left), hop(2, y, 1, right), hop(3, y, 0, left)]
        for copy in ring:
            copy.start()
        hop(0, up, 0, right).wait_recv()
        ring.append(hop(4, up, 0, right))
        ring[4].start()
        hop(1, down, 1, left).wait_recv()
        ring.append(hop(5, down, 1, left))
        ring[5].start()
        hop(2, up, 1, right).wait_recv()
        hop(3, down, 0, left).wait_recv()
        hop(4, far, 0, right).wait_recv()
        hop(5, far, 1, left).wait_recv()
        for k in range(4):
            keys[0, 192 + 64 * k:256 + 64 * k, :] = slabs[lax.rem(y + k, 4)]
    else:
        for c in range(4):
            own_scores(c)
        keys[0, 192:448, :] = trunk_ref[...]
    keys[1, 192:448, :] = pltpu.roll(keys[0, 192:448, :].astype(F32), 64, 1).astype(BF16)
    live = jnp.where(iota((256, 1), 0) % 32 < cnt_ref[leaf], 0.0, -1e30)

    def far_scores(c):
        u, par = chunks[c]
        return (dot(keys[par, 192:448, :], q_of(u, par), 1, 1) + live,
                dot(keys[0, 192:448, 0:512], do_of(u, par), 1, 1))

    ahead = far_scores(0)
    for c in range(4):
        u, par = chunks[c]
        sf, dpf = ahead
        if c < 3:
            ahead = far_scores(c + 1)
        so, dpo = sown[c], dpown[c]
        m = jnp.maximum(jnp.max(sf, axis=0, keepdims=True), jnp.max(so, axis=0, keepdims=True))
        ef = jnp.exp2((sf - m) * (SCALE * LOG2E))
        eo = jnp.exp2((so - m) * (SCALE * LOG2E))
        inv = 1.0 / (jnp.sum(ef, axis=0, keepdims=True) + jnp.sum(eo, axis=0, keepdims=True))
        pf, po = ef * inv, eo * inv
        delta = jnp.sum(pf * dpf, axis=0, keepdims=True) + jnp.sum(po * dpo, axis=0, keepdims=True)
        dsf = (pf * (dpf - delta)).astype(BF16)
        ds[c, 192:448, :] = dsf
        ds[c, 0:192, :] = (po * (dpo - delta)).astype(BF16)
        p_own[c] = po.astype(BF16)
        dk = dot(dsf, q_of(u, par), 1, 0)
        dv = dot(pf.astype(BF16), do_of(u, par), 1, 0)
        if u == 0:
            acc_k[par, 192:448, :] = dk
        else:
            acc_k[par, 192:448, :] += dk
        if c == 0:
            acc_v[192:448, :] = dv
        else:
            acc_v[192:448, :] += dv

    def merged(lo, n):
        dk = (acc_k[0, lo:lo + n, :] + pltpu.roll(acc_k[1, lo:lo + n, :], 576, 1)) * SCALE
        return jnp.concatenate([dk[:, 0:512] + acc_v[lo:lo + n, :], dk[:, 512:WIDE]], axis=1)

    for k in range(4):
        for half in range(2):
            x_far[k, half] = merged(192 + 64 * k + 32 * half, 32).astype(BF16)

    def ring_start(x, mid, send_sem, recv_sem):
        copies = [
            remote(x(2, 0), mid.at[0], send_sem.at[0], recv_sem.at[0], right),
            remote(x(2, 1), mid.at[1], send_sem.at[1], recv_sem.at[1], left),
            remote(x(1, 1), mid.at[2], send_sem.at[2], recv_sem.at[2], right),
            remote(x(3, 0), mid.at[3], send_sem.at[3], recv_sem.at[3], left),
        ]
        for copy in copies:
            copy.start()
        return copies

    def ring_pass(copies, value, mid, through, send_sem, recv_sem):
        for side, k in ((0, 1), (1, 3)):
            copies[side].wait_recv()
            through[side] = (value(k, side) + mid[side].astype(F32)).astype(BF16)
            copy = remote(through.at[side], mid.at[4 + side], send_sem.at[4 + side], recv_sem.at[4 + side],
                          (right, left)[side])
            copy.start()
            copies.append(copy)

    def ring_sum(copies, value, mid):
        for k in range(2, 6):
            copies[k].wait_recv()
        return [value(0, half) + mid[4 + half].astype(F32) + mid[3 - half].astype(F32) for half in range(2)]

    if comm:
        far_copies = ring_start(lambda k, half: x_far.at[k, half], r_far, far_send, far_recv)

    for c in range(4):
        u, par = chunks[c]
        dk = dot(ds[c, 0:192, :], q_of(u, par), 1, 0)
        dv = dot(p_own[c], do_of(u, par), 1, 0)
        if u == 0:
            acc_k[par, 0:192, :] = dk
        else:
            acc_k[par, 0:192, :] += dk
        if c == 0:
            acc_v[0:192, :] = dv
        else:
            acc_v[0:192, :] += dv
    for h in range(8):
        x_own[h] = merged(24 * h, 24).astype(BF16)

    def far_value(k, half):
        return x_far[k, half].astype(F32)

    def own_at(k, half):
        return half * 4 + lax.rem(y + k, 4)

    def own_value(k, half):
        return x_own[own_at(k, half)].astype(F32)

    def d_query(u):
        grads = [dot(ds[2 * u + par], keys[par], 0, 0) * SCALE for par in range(2)]
        for n in range(4):
            r = slice(192 * n, 192 * n + 192)
            at = 1152 * n
            dq_out[u, :, at:at + 512] = grads[0][r, 0:512].astype(BF16)
            dq_out[u, :, at + 512:at + 640] = (grads[0][r, 512:640] + grads[1][r, 0:128]).astype(BF16)
            dq_out[u, :, at + 640:at + 1152] = grads[1][r, 128:640].astype(BF16)
        copy = pltpu.make_async_copy(dq_out.at[u], dq_hbm.at[:, pl.ds(4608 * u, 4608)], store_sem.at[u])
        copy.start()
        return copy

    if comm:
        ring_pass(far_copies, far_value, r_far, m_far, far_send, far_recv)
        own_copies = ring_start(lambda k, half: x_own.at[own_at(k, half)], r_own, own_send, own_recv)
        stores = [d_query(0)]
        sums = ring_sum(far_copies, far_value, r_far)
        rows = dot(spread, jnp.concatenate(sums, axis=0).astype(BF16), 0, 0)
        for d in range(2 * LEAF):
            t_out[d] = rows[2 * d:2 * d + 2].astype(BF16)

        def send_rows(k, c):
            to = lax.rem(me + k, 2 * LEAF)
            remote(t_out.at[to], t_got.at[me], t_send.at[k], t_recv.at[me], plane(to)).start()
            return c

        lax.fori_loop(1, 2 * LEAF, send_rows, 0)
        mine = pltpu.make_async_copy(t_out.at[me], t_got.at[me], t_recv.at[me])
        mine.start()
        ring_pass(own_copies, own_value, r_own, m_own, own_send, own_recv)
        stores.append(d_query(1))
        sums = ring_sum(own_copies, own_value, r_own)
        for half in range(2):
            pair[half] = sums[half]
        pair_out = remote(pair.at[1 - deep], pair_in, pair_sem.at[0], pair_sem.at[1], {"head": (1 - deep) * 4 + y})
        pair_out.start()
        mine.wait()

        def receive_rows(k, c):
            source = lax.rem(me + k, 2 * LEAF)
            remote(t_out.at[source], t_got.at[source], t_send.at[k], t_recv.at[source], plane(source)).wait()
            return c

        lax.fori_loop(1, 2 * LEAF, receive_rows, 0)
        for d in range(2 * LEAF):
            t_tall[2 * d:2 * d + 2, :] = t_got[d].astype(F32)
        spare_ref[...] = dot(collect, t_tall[...].astype(BF16), 0, 0)[:, 0:576]
        pair_out.wait()
        branch_ref[...] = (pair[deep] + pair_in[...])[:, 0:576]
        for copy in ring + far_copies + own_copies:
            copy.wait_send()
    else:
        stores = [d_query(0), d_query(1)]
        spare_ref[...] = x_far[...]
        branch_ref[...] = x_own[...]
    for copy in stores:
        copy.wait()


def fused_call(comm, ancestors, count, own, trunk, q, do):
    if comm:
        small = (jax.ShapeDtypeStruct((24, 576), F32), jax.ShapeDtypeStruct((16, 576), F32))
    else:
        small = (jax.ShapeDtypeStruct((8, 24, WIDE), BF16), jax.ShapeDtypeStruct((4, 2, 32, WIDE), BF16))
    vmem, hbm = pl.BlockSpec(memory_space=pltpu.VMEM), pl.BlockSpec(memory_space=pl.ANY)
    dma = pltpu.SemaphoreType.DMA
    return pl.pallas_call(
        functools.partial(fused, comm),
        out_shape=(jax.ShapeDtypeStruct((192, 9216), BF16),) + small,
        in_specs=[vmem, pl.BlockSpec(memory_space=pltpu.SMEM), vmem, vmem, hbm, hbm],
        out_specs=(hbm, vmem, vmem),
        scratch_shapes=[
            pltpu.VMEM((2, 1536, WIDE), BF16),
            pltpu.VMEM((2, 1536, 512), BF16),
            pltpu.VMEM((2, 448, WIDE), BF16),
            pltpu.VMEM((4, 192, 768), F32),
            pltpu.VMEM((4, 192, 768), F32),
            pltpu.VMEM((4, 192, 768), BF16),
            pltpu.VMEM((4, 448, 768), BF16),
            pltpu.VMEM((2, 448, WIDE), F32),
            pltpu.VMEM((448, 512), F32),
            pltpu.VMEM((2, 192, 4608), BF16),
            pltpu.VMEM((LEAF, 4, WIDE), BF16),
            pltpu.VMEM((LEAF, 4, WIDE), BF16),
            pltpu.VMEM((128, WIDE), F32),
            pltpu.VMEM((4, 64, WIDE), BF16),
            pltpu.VMEM((4, 2, 32, WIDE), BF16),
            pltpu.VMEM((8, 24, WIDE), BF16),
            pltpu.VMEM((6, 32, WIDE), BF16),
            pltpu.VMEM((6, 24, WIDE), BF16),
            pltpu.VMEM((2, 32, WIDE), BF16),
            pltpu.VMEM((2, 24, WIDE), BF16),
            pltpu.VMEM((2, 24, WIDE), F32),
            pltpu.VMEM((24, WIDE), F32),
            pltpu.VMEM((2 * LEAF, 2, WIDE), BF16),
            pltpu.VMEM((2 * LEAF, 2, WIDE), BF16),
            pltpu.VMEM((128, WIDE), F32),
            dma((32,)), dma((2,)), dma((LEAF,)), dma((LEAF,)), dma((6,)), dma((6,)), dma((6,)), dma((6,)),
            dma((6,)), dma((6,)), dma((2,)), dma((2 * LEAF,)), dma((2 * LEAF,)),
        ],
        compiler_params=pltpu.CompilerParams(collective_id=0, has_side_effects=True) if comm else None,
        name="backward",
    )(ancestors, count, own, trunk, q, do)


def local(queries, d_out, branch_latent, trunk_latent, ancestors, anc_count):
    d_queries, d_branch, d_trunk = fused_call(True, ancestors, anc_count, branch_latent, trunk_latent, queries, d_out)
    return d_queries, d_branch, d_trunk[:, None, :]


def solution(mesh):
    return jax.shard_map(
        local,
        mesh=mesh,
        in_specs=(P("leaf", "head"), P("leaf", "head"), P("leaf", None), P("leaf", None, None), P(), P()),
        out_specs=(P("leaf", "head"), P(("leaf", "head"), None), P("leaf", "head", None)),
        check_vma=False,
    )
```

time: 436 us -> 58.2 us (0.13)
  waiting for transfers between devices: 351 us -> 0 us
  Pallas kernels: 0 us -> 51.3 us
  local copies, waits for them, and re-layouts: 34.1 us -> 6.09 us
  other arithmetic: 20.3 us -> 0 us
  matrix products: 16.1 us -> 0 us
  between operations: 13.9 us -> 0.64 us
    reduce_scatter x2 -> x0, waiting for transfers between devices: 212 us -> none  [the longest x1 137 us: local(): lax.psum_scatter(spread.astype(jnp.bfloat16), 'leaf', scatter_dimension=0...]
    unnamed x5 -> x0, waiting for transfers between devices: 82.3 us -> none
    all_gather x1 -> x0, waiting for transfers between devices: 56.7 us -> none  [local(): everything = lax.all_gather(trunk_latent, 'leaf', axis=0, tiled=True)]
    pallas_call x0 -> x1, Pallas kernels: none -> 51.3 us  [fused_call(): pl.pallas_call(functools.partial(fused, comm), out_shape=(jax.ShapeDtypeS...]
    dot_general x5 -> x0, matrix products: 16.1 us -> none  [the longest x1 4.8 us: local(): jnp.einsum('thc,kc->htk', query_heads, key_rows, preferred_element_type=j...]
    reshape x2 -> x0, local copies, waits for them, and re-layouts: 14.1 us -> none  [the longest x1 7.03 us: local(): query_heads = queries.reshape(tok_rows, heads_here, LATENT)]
    convert_element_type x2 -> x0, other arithmetic: 8.13 us -> none  [the longest x1 6.89 us: local(): spread.astype(jnp.bfloat16)]
    scatter-add x1 -> x0, other arithmetic: 4.95 us -> none  [local(): spread = jnp.zeros((trunk_count * leaf_count, grad_rows, LATENT), jnp.flo...]
  transfers between devices with their start and end apart: 4 -> 0, of which waited for: 4 -> 0; matrix products, arithmetic and copies ran while one was open for 7% -> 0% of each run, Pallas kernels for 0% -> 0%
where the time goes in v2:
time: 58.2 us; the launch traced here: 58.1 us
  Pallas kernels  51.3 us (88%)
  local copies, waits for them, and re-layouts  6.09 us (10%)
  between operations  0.64 us (1%)
    pallas_call x1, Pallas kernels, fused_call(): pl.pallas_call(functools.partial(fused, comm), out_shape=(jax.ShapeDtypeS...  51.3 us
    unnamed x5, local copies, waits for them, and re-layouts  6.09 us

profile of v2, /device:TPU:6, one launch (start us, length us, event | category | flops | bytes accessed | tf_op | source)
XLA Modules:
  0.0 58.1 jit_solution(8269775092088744886)
XLA Ops:
  0.6 51.3 %backward.1 = (bf16[192,9216]{1,0:T(8,128)(2,1)}, f32[24,576]{1,0:T(8,128)}, f32[16,576]{1,0:T(8,128)}) custom-call(s32[32,32]{1,0:T(8,128)} %anc_ref.1, s32[32]{0:T(128)} %cnt_ref.1, bf16[192,576]{1,0:T(8,128)(2,1)} %own_ref.1, bf16[16,8,576]{2,1,0:T(8,128)(2,1)} %trunk_ref.1, bf16[192,9216]{1,0:T(8,128)(2,1)} %q_hbm.1, bf16[192,8192]{1,0:T(8,128)(2,1)} %do_hbm.1), custom_call_target="tpu_custom_call" | custom-call | tf_op jit(solution)/shard_map/backward/pallas_call | solution.py:350
  52.0 1.4 %copy.9 = f32[16,1,576]{2,1,0:T(1,128)} copy(f32[16,1,576]{2,0,1:T(8,128)} %bitcast.1) | data formatting | bytes 73728
  53.4 0.0 copy-start
  53.4 4.0 %copy.12 = bf16[192,9216]{1,0:T(8,128)(2,1)} copy(bf16[192,9216]{1,0:T(8,128)(2,1)} %get-tuple-element.15) | data formatting | bytes 7077888
  57.4 0.0 copy-done
  57.4 0.6 %copy.13 = f32[24,576]{1,0:T(8,128)} copy(f32[24,576]{1,0:T(8,128)S(1)} %copy-done) | data formatting | bytes 110592
Async XLA Ops:
  53.4 4.0 %copy-start = (f32[24,576]{1,0:T(8,128)S(1)}, f32[24,576]{1,0:T(8,128)}, u32[]{:S(2)}) copy-start(f32[24,576]{1,0:T(8,128)} %get-tuple-element.16) | copy-start | bytes 165892

commit v3 on v2

--- a/solution.py
+++ b/solution.py
@@ -11,6 +11,7 @@
 SCALE = float(192) ** -0.5
 LOG2E = 1.4426950408889634
 LEAF = 32
+VMEM_LIMIT = 50 * 2**20
 WIDE = 640
 
 
@@ -53,11 +54,20 @@
     pl.semaphore_signal(sem, inc=1, device_id=where, device_id_type=pl.DeviceIdType.MESH)
 
 
-def fused(comm, anc_ref, cnt_ref, own_ref, trunk_ref, q_hbm, do_hbm, dq_hbm, branch_ref, spare_ref,
-          qs, dos, keys, sown, dpown, p_own, ds, acc_k, acc_v, dq_out,
-          g_out, g_got, g_tall, slabs, x_far, x_own, r_far, r_own, m_far, m_own, pair, pair_in, t_out, t_got, t_tall,
-          load_sem, store_sem, g_send, g_recv, ring_send, ring_recv, far_send, far_recv, own_send, own_recv,
+def fused(comm, anc_hbm, cnt_hbm, own_hbm, trunk_hbm, q_hbm, do_hbm, dq_ref, branch_ref, spare_ref, collect_ref,
+          anc_ref, cnt_ref, own_ref, trunk_ref, small_sem,
+          qs, dos, keys, sown, dpown, p_own, ds, acc_k, acc_v,
+          g_out, g_got, g_tall, slabs, x_far, x_own, r_far, r_own, m_far, m_own, pair, pair_in, t_out, t_got,
+          load_sem, g_send, g_recv, ring_send, ring_recv, far_send, far_recv, own_send, own_recv,
           pair_sem, t_send, t_recv):
+    small = [
+        pltpu.make_async_copy(anc_hbm, anc_ref, small_sem.at[0]),
+        pltpu.make_async_copy(trunk_hbm, trunk_ref, small_sem.at[1]),
+        pltpu.make_async_copy(own_hbm, own_ref, small_sem.at[2]),
+        pltpu.make_async_copy(cnt_hbm, cnt_ref, small_sem.at[3]),
+    ]
+    for copy in small:
+        copy.start()
     if comm:
         leaf, head = lax.axis_index("leaf"), lax.axis_index("head")
         deep, y = head // 4, lax.rem(head, 4)
@@ -103,6 +113,8 @@
     def do_of(u, par):
         return dos[par, 768 * u:768 * u + 768, :]
 
+    for copy in small:
+        copy.wait()
     if comm:
         i = iota((128, 1), 0)
         block = listed_block(anc_ref[...], leaf, i // 4, (i // 2) % 2)
@@ -120,7 +132,7 @@
         spread = jnp.where(want == iota((64, 128), 1).astype(F32), 1.0, 0.0).astype(BF16)
         i = iota((128, 1), 0)
         block = listed_block(anc_ref[...], leaf, (i // 2) % 32, i % 2)
-        collect = jnp.where(block - 1.0 == iota((128, 16), 1).astype(F32), 1.0, 0.0).astype(BF16)
+        collect_ref[...] = jnp.where(block - 1.0 == iota((128, 128), 1).astype(F32), 1.0, 0.0)
 
     own = own_ref[...]
     blank = jnp.zeros((192, 64), BF16)
@@ -257,7 +269,7 @@
     if comm:
         far_copies = ring_start(lambda k, half: x_far.at[k, half], r_far, far_send, far_recv)
 
-    for c in range(4):
+    def own_keys(c):
         u, par = chunks[c]
         dk = dot(ds[c, 0:192, :], q_of(u, par), 1, 0)
         dv = dot(p_own[c], do_of(u, par), 1, 0)
@@ -269,8 +281,10 @@
             acc_v[0:192, :] = dv
         else:
             acc_v[0:192, :] += dv
-    for h in range(8):
-        x_own[h] = merged(24 * h, 24).astype(BF16)
+
+    def own_done():
+        for h in range(8):
+            x_own[h] = merged(24 * h, 24).astype(BF16)
 
     def far_value(k, half):
         return x_far[k, half].astype(F32)
@@ -282,36 +296,42 @@
         return x_own[own_at(k, half)].astype(F32)
 
     def d_query(u):
-        grads = [dot(ds[2 * u + par], keys[par], 0, 0) * SCALE for par in range(2)]
+        even = dot(ds[2 * u], keys[0], 0, 0) * SCALE
+        odd = dot(ds[2 * u + 1], keys[1], 0, 0) * SCALE
         for n in range(4):
             r = slice(192 * n, 192 * n + 192)
-            at = 1152 * n
-            dq_out[u, :, at:at + 512] = grads[0][r, 0:512].astype(BF16)
-            dq_out[u, :, at + 512:at + 640] = (grads[0][r, 512:640] + grads[1][r, 0:128]).astype(BF16)
-            dq_out[u, :, at + 640:at + 1152] = grads[1][r, 128:640].astype(BF16)
-        copy = pltpu.make_async_copy(dq_out.at[u], dq_hbm.at[:, pl.ds(4608 * u, 4608)], store_sem.at[u])
-        copy.start()
-        return copy
-
-    if comm:
+            at = 4608 * u + 1152 * n
+            dq_ref[:, at:at + 512] = even[r, 0:512].astype(BF16)
+            dq_ref[:, at + 512:at + 640] = (even[r, 512:640] + odd[r, 0:128]).astype(BF16)
+            dq_ref[:, at + 640:at + 1152] = odd[r, 128:640].astype(BF16)
+
+    if comm:
+        for c in range(3):
+            own_keys(c)
         ring_pass(far_copies, far_value, r_far, m_far, far_send, far_recv)
+        own_keys(3)
+        own_done()
         own_copies = ring_start(lambda k, half: x_own.at[own_at(k, half)], r_own, own_send, own_recv)
-        stores = [d_query(0)]
         sums = ring_sum(far_copies, far_value, r_far)
         rows = dot(spread, jnp.concatenate(sums, axis=0).astype(BF16), 0, 0)
         for d in range(2 * LEAF):
             t_out[d] = rows[2 * d:2 * d + 2].astype(BF16)
 
-        def send_rows(k, c):
+        def far_first(j):
+            return lax.rem(j + 24, 2 * LEAF - 1) + 1
+
+        def send_rows(j, c):
+            k = far_first(j)
             to = lax.rem(me + k, 2 * LEAF)
             remote(t_out.at[to], t_got.at[me], t_send.at[k], t_recv.at[me], plane(to)).start()
             return c
 
-        lax.fori_loop(1, 2 * LEAF, send_rows, 0)
+        lax.fori_loop(0, 2 * LEAF - 1, send_rows, 0)
         mine = pltpu.make_async_copy(t_out.at[me], t_got.at[me], t_recv.at[me])
         mine.start()
+        d_query(0)
         ring_pass(own_copies, own_value, r_own, m_own, own_send, own_recv)
-        stores.append(d_query(1))
+        d_query(1)
         sums = ring_sum(own_copies, own_value, r_own)
         for half in range(2):
             pair[half] = sums[half]
@@ -326,33 +346,39 @@
 
         lax.fori_loop(1, 2 * LEAF, receive_rows, 0)
         for d in range(2 * LEAF):
-            t_tall[2 * d:2 * d + 2, :] = t_got[d].astype(F32)
-        spare_ref[...] = dot(collect, t_tall[...].astype(BF16), 0, 0)[:, 0:576]
+            spare_ref[2 * d:2 * d + 2, :] = t_got[d].astype(F32)
         pair_out.wait()
-        branch_ref[...] = (pair[deep] + pair_in[...])[:, 0:576]
+        branch_ref[...] = pair[deep] + pair_in[...]
         for copy in ring + far_copies + own_copies:
             copy.wait_send()
     else:
-        stores = [d_query(0), d_query(1)]
+        for c in range(4):
+            own_keys(c)
+        own_done()
+        d_query(0)
+        d_query(1)
         spare_ref[...] = x_far[...]
         branch_ref[...] = x_own[...]
-    for copy in stores:
-        copy.wait()
 
 
 def fused_call(comm, ancestors, count, own, trunk, q, do):
     if comm:
-        small = (jax.ShapeDtypeStruct((24, 576), F32), jax.ShapeDtypeStruct((16, 576), F32))
+        small = (pltpu.VMEM((24, WIDE), F32), pltpu.VMEM((128, WIDE), F32))
     else:
-        small = (jax.ShapeDtypeStruct((8, 24, WIDE), BF16), jax.ShapeDtypeStruct((4, 2, 32, WIDE), BF16))
-    vmem, hbm = pl.BlockSpec(memory_space=pltpu.VMEM), pl.BlockSpec(memory_space=pl.ANY)
+        small = (pltpu.VMEM((8, 24, WIDE), BF16), pltpu.VMEM((4, 2, 32, WIDE), BF16))
+    vmem, hbm = pl.BlockSpec(memory_space=pltpu.VMEM), pl.BlockSpec(memory_space=pltpu.HBM)
     dma = pltpu.SemaphoreType.DMA
     return pl.pallas_call(
         functools.partial(fused, comm),
-        out_shape=(jax.ShapeDtypeStruct((192, 9216), BF16),) + small,
-        in_specs=[vmem, pl.BlockSpec(memory_space=pltpu.SMEM), vmem, vmem, hbm, hbm],
-        out_specs=(hbm, vmem, vmem),
+        out_shape=(pltpu.VMEM((192, 9216), BF16),) + small + (pltpu.VMEM((128, 128), F32),),
+        in_specs=[hbm] * 6,
+        out_specs=(vmem,) * 4,
         scratch_shapes=[
+            pltpu.VMEM((LEAF, LEAF), jnp.int32),
+            pltpu.SMEM(count.shape, jnp.int32),
+            pltpu.VMEM(own.shape, BF16),
+            pltpu.VMEM(trunk.shape, BF16),
+            dma((4,)),
             pltpu.VMEM((2, 1536, WIDE), BF16),
             pltpu.VMEM((2, 1536, 512), BF16),
             pltpu.VMEM((2, 448, WIDE), BF16),
@@ -362,7 +388,6 @@
             pltpu.VMEM((4, 448, 768), BF16),
             pltpu.VMEM((2, 448, WIDE), F32),
             pltpu.VMEM((448, 512), F32),
-            pltpu.VMEM((2, 192, 4608), BF16),
             pltpu.VMEM((LEAF, 4, WIDE), BF16),
             pltpu.VMEM((LEAF, 4, WIDE), BF16),
             pltpu.VMEM((128, WIDE), F32),
@@ -377,18 +402,50 @@
             pltpu.VMEM((24, WIDE), F32),
             pltpu.VMEM((2 * LEAF, 2, WIDE), BF16),
             pltpu.VMEM((2 * LEAF, 2, WIDE), BF16),
-            pltpu.VMEM((128, WIDE), F32),
-            dma((32,)), dma((2,)), dma((LEAF,)), dma((LEAF,)), dma((6,)), dma((6,)), dma((6,)), dma((6,)),
+            dma((32,)), dma((LEAF,)), dma((LEAF,)), dma((6,)), dma((6,)), dma((6,)), dma((6,)),
             dma((6,)), dma((6,)), dma((2,)), dma((2 * LEAF,)), dma((2 * LEAF,)),
         ],
-        compiler_params=pltpu.CompilerParams(collective_id=0, has_side_effects=True) if comm else None,
+        compiler_params=pltpu.CompilerParams(
+            collective_id=0, has_side_effects=True, vmem_limit_bytes=VMEM_LIMIT
+        ) if comm else pltpu.CompilerParams(vmem_limit_bytes=VMEM_LIMIT),
         name="backward",
     )(ancestors, count, own, trunk, q, do)
 
 
+def finish(grad_ref, rows_ref, sum_ref, collect_ref, dq_hbm, branch_ref, trunk_ref, sem):
+    copies = []
+    for k in range(4):
+        part = pl.ds(48 * k, 48)
+        copies.append(pltpu.make_async_copy(grad_ref.at[part], dq_hbm.at[part], sem.at[k]))
+        copies[k].start()
+    branch_ref[...] = sum_ref[:, 0:576]
+    total = dot(collect_ref[...].astype(BF16), rows_ref[...].astype(BF16), 0, 0)
+    for b in range(16):
+        trunk_ref[b] = total[b:b + 1, 0:576]
+    for copy in copies:
+        copy.wait()
+
+
+def finish_call(grad, rows, total, collect):
+    vmem, hbm = pl.BlockSpec(memory_space=pltpu.VMEM), pl.BlockSpec(memory_space=pl.ANY)
+    return pl.pallas_call(
+        finish,
+        out_shape=(
+            jax.ShapeDtypeStruct((192, 9216), BF16),
+            jax.ShapeDtypeStruct((24, 576), F32),
+            jax.ShapeDtypeStruct((16, 1, 576), F32),
+        ),
+        in_specs=[vmem] * 4,
+        out_specs=(hbm, vmem, vmem),
+        scratch_shapes=[pltpu.SemaphoreType.DMA((4,))],
+        compiler_params=pltpu.CompilerParams(vmem_limit_bytes=16 * 2**20),
+        name="finish",
+    )(grad, rows, total, collect)
+
+
 def local(queries, d_out, branch_latent, trunk_latent, ancestors, anc_count):
-    d_queries, d_branch, d_trunk = fused_call(True, ancestors, anc_count, branch_latent, trunk_latent, queries, d_out)
-    return d_queries, d_branch, d_trunk[:, None, :]
+    grad, total, rows, collect = fused_call(True, ancestors, anc_count, branch_latent, trunk_latent, queries, d_out)
+    return finish_call(grad, rows, total, collect)
 
 
 def solution(mesh):

time: 58.2 us -> 55.9 us (0.960)
  local copies, waits for them, and re-layouts: 6.09 us -> 1.37 us
  Pallas kernels: 51.3 us -> 53.7 us
    unnamed x5 -> x4, local copies, waits for them, and re-layouts: 6.09 us -> 1.37 us
    pallas_call x1 -> x2, Pallas kernels: 51.3 us -> 53.7 us  [the longest x1 51.2 us: fused_call(): pl.pallas_call(functools.partial(fused, comm), out_shape=(pltpu.VMEM((192...]
where the time goes in v3:
time: 55.9 us; the launch traced here: 55.7 us
  Pallas kernels  53.7 us (96%)
  local copies, waits for them, and re-layouts  1.37 us (2%)
  between operations  0.65 us (1%)
    pallas_call x1, Pallas kernels, fused_call(): pl.pallas_call(functools.partial(fused, comm), out_shape=(pltpu.VMEM((192...  51.2 us
    pallas_call x1, Pallas kernels, finish_call(): pl.pallas_call(finish, out_shape=(jax.ShapeDtypeStruct((192, 9216), BF16)...  2.48 us
    unnamed x4, local copies, waits for them, and re-layouts  1.37 us

profile of v3, /device:TPU:6, one launch (start us, length us, event | category | flops | bytes accessed | tf_op | source)
XLA Modules:
  0.0 55.7 jit_solution(4158252010205897618)
XLA Ops:
  0.6 0.0 copy-start
  0.6 0.7 %copy-done = s32[32,32]{1,0:T(8,128)S(1)} copy-done((s32[32,32]{1,0:T(8,128)S(1)}, s32[32,32]{1,0:T(8,128)}, u32[]{:S(2)}) %copy-start) | copy-done | bytes 4120
  1.4 0.0 copy-start.1
  1.4 0.7 %copy-done.1 = s32[32]{0:T(128)S(1)} copy-done((s32[32]{0:T(128)S(1)}, s32[32]{0:T(128)}, u32[]{:S(2)}) %copy-start.1) | copy-done | bytes 152
  2.0 51.2 %backward.1 = (bf16[192,9216]{1,0:T(8,128)(2,1)S(1)}, f32[24,640]{1,0:T(8,128)S(1)}, f32[128,640]{1,0:T(8,128)S(1)}, f32[128,128]{1,0:T(8,128)S(1)}) custom-call(s32[32,32]{1,0:T(8,128)S(1)} %copy-done, s32[32]{0:T(128)S(1)} %copy-done.1, bf16[192,576]{1,0:T(8,128)(2,1)} %own_hbm.1, bf16[16,8,576]{2,1,0:T(8,128)(2,1)} %trunk_hbm.1, bf16[192,9216]{1,0:T(8,128)(2,1)} %q_hbm.1, ...), custom_call_target="tpu_custom_call" | custom-call | tf_op jit(solution)/shard_map/backward/pallas_call | solution.py:371
  53.2 2.5 %finish.1 = (bf16[192,9216]{1,0:T(8,128)(2,1)}, f32[24,576]{1,0:T(8,128)}, f32[16,1,576]{2,1,0:T(1,128)}) custom-call(bf16[192,9216]{1,0:T(8,128)(2,1)S(1)} %get-tuple-element.7.grad_ref, f32[128,640]{1,0:T(8,128)S(1)} %get-tuple-element.8.rows_ref, f32[24,640]{1,0:T(8,128)S(1)} %get-tuple-element.9.sum_ref, f32[128,128]{1,0:T(8,128)S(1)} %get-tuple-element.10.collect_ref), custom_call_target="tpu_custom_call" | custom-call | tf_op jit(solution)/shard_map/finish/pallas_call | solution.py:431
Async XLA Ops:
  0.6 0.7 %copy-start = (s32[32,32]{1,0:T(8,128)S(1)}, s32[32,32]{1,0:T(8,128)}, u32[]{:S(2)}) copy-start(s32[32,32]{1,0:T(8,128)} %anc_hbm.1) | copy-start | bytes 12292
  1.4 0.7 %copy-start.1 = (s32[32]{0:T(128)S(1)}, s32[32]{0:T(128)}, u32[]{:S(2)}) copy-start(s32[32]{0:T(128)} %cnt_hbm.1) | copy-start | bytes 388

commit v4 on v3

--- a/solution.py
+++ b/solution.py
@@ -56,9 +56,9 @@
 
 def fused(comm, anc_hbm, cnt_hbm, own_hbm, trunk_hbm, q_hbm, do_hbm, dq_ref, branch_ref, spare_ref, collect_ref,
           anc_ref, cnt_ref, own_ref, trunk_ref, small_sem,
-          qs, dos, keys, sown, dpown, p_own, ds, acc_k, acc_v,
+          qs, dos, keys, sown, dpown, p_own, ds, acc_k, acc_v, dq_out,
           g_out, g_got, g_tall, slabs, x_far, x_own, r_far, r_own, m_far, m_own, pair, pair_in, t_out, t_got,
-          load_sem, g_send, g_recv, ring_send, ring_recv, far_send, far_recv, own_send, own_recv,
+          load_sem, store_sem, g_send, g_recv, ring_send, ring_recv, far_send, far_recv, own_send, own_recv,
           pair_sem, t_send, t_recv):
     small = [
         pltpu.make_async_copy(anc_hbm, anc_ref, small_sem.at[0]),
@@ -75,16 +75,21 @@
         right = {"head": deep * 4 + lax.rem(y + 1, 4)}
         left = {"head": deep * 4 + lax.rem(y + 3, 4)}
 
-        def plane(p):
-            return {"leaf": lax.rem(p, LEAF), "head": (p // LEAF) * 4 + y}
+        here, there = deep * LEAF, (1 - deep) * LEAF
+        across = (1 - deep) * 4 + y
 
         barrier = pltpu.get_barrier_semaphore()
 
+        def greet_across(k, c):
+            signal(barrier, {"leaf": k, "head": across})
+            return c
+
         def greet(k, c):
-            signal(barrier, plane(lax.rem(me + k, 2 * LEAF)))
-            return c
-
-        lax.fori_loop(1, 2 * LEAF, greet, 0)
+            signal(barrier, {"leaf": lax.rem(leaf + k, LEAF)})
+            return c
+
+        lax.fori_loop(0, LEAF, greet_across, 0)
+        lax.fori_loop(1, LEAF, greet, 0)
         signal(barrier, left)
         signal(barrier, right)
     else:
@@ -124,6 +129,26 @@
         rows = dot(pick, jnp.concatenate([trunk, jnp.zeros((128, WIDE - 576), BF16)], axis=1), 1, 0)
         for b in range(LEAF):
             g_out[b] = rows[4 * b:4 * b + 4].astype(BF16)
+
+    def own_scores(c, causal):
+        for copy in loads[chunks[c]]:
+            copy.wait()
+        u, par = chunks[c]
+        s = dot(keys[par, 0:192, :], q_of(u, par), 1, 1)
+        sown[c] = s + jnp.concatenate([causal] * 4, axis=1)
+        dpown[c] = dot(keys[0, 0:192, 0:512], do_of(u, par), 1, 1)
+
+    if comm:
+        pl.semaphore_wait(barrier, 2 * LEAF + 1)
+
+        def send(k, c):
+            to = lax.rem(leaf + k, LEAF)
+            remote(g_out.at[to], g_got.at[leaf], g_send.at[k], g_recv.at[leaf], {"leaf": to}).start()
+            return c
+
+        lax.fori_loop(1, LEAF, send, 0)
+        mine = pltpu.make_async_copy(g_out.at[leaf], g_got.at[leaf], g_recv.at[leaf])
+        mine.start()
         i = iota((64, 1), 0)
         owner, rank = owner_and_rank(anc_ref[pl.ds(leaf, 1), :], i % 32)
         want = owner * 4.0 + rank * 2.0 + (i // 32).astype(F32)
@@ -133,34 +158,13 @@
         i = iota((128, 1), 0)
         block = listed_block(anc_ref[...], leaf, (i // 2) % 32, i % 2)
         collect_ref[...] = jnp.where(block - 1.0 == iota((128, 128), 1).astype(F32), 1.0, 0.0)
-
-    own = own_ref[...]
-    blank = jnp.zeros((192, 64), BF16)
-    keys[0, 0:192, :] = jnp.concatenate([own, blank], axis=1)
-    keys[1, 0:192, :] = pltpu.roll(jnp.concatenate([own, blank], axis=1).astype(F32), 64, 1).astype(BF16)
-    causal = jnp.where(iota((192, 192), 0) <= iota((192, 192), 1), 0.0, -1e30)
-
-    def own_scores(c):
-        for copy in loads[chunks[c]]:
-            copy.wait()
-        u, par = chunks[c]
-        s = dot(keys[par, 0:192, :], q_of(u, par), 1, 1)
-        sown[c] = s + jnp.concatenate([causal] * 4, axis=1)
-        dpown[c] = dot(keys[0, 0:192, 0:512], do_of(u, par), 1, 1)
-
-    if comm:
-        pl.semaphore_wait(barrier, 2 * LEAF + 1)
-
-        def send(k, c):
-            to = lax.rem(leaf + k, LEAF)
-            remote(g_out.at[to], g_got.at[leaf], g_send.at[k], g_recv.at[leaf], {"leaf": to}).start()
-            return c
-
-        lax.fori_loop(1, LEAF, send, 0)
-        mine = pltpu.make_async_copy(g_out.at[leaf], g_got.at[leaf], g_recv.at[leaf])
-        mine.start()
+        own = own_ref[...]
+        blank = jnp.zeros((192, 64), BF16)
+        keys[0, 0:192, :] = jnp.concatenate([own, blank], axis=1)
+        keys[1, 0:192, :] = pltpu.roll(jnp.concatenate([own, blank], axis=1).astype(F32), 64, 1).astype(BF16)
+        causal = jnp.where(iota((192, 192), 0) <= iota((192, 192), 1), 0.0, -1e30)
         for c in range(4):
-            own_scores(c)
+            own_scores(c, causal)
         mine.wait()
 
         def receive(k, c):
@@ -194,8 +198,13 @@
         for k in range(4):
             keys[0, 192 + 64 * k:256 + 64 * k, :] = slabs[lax.rem(y + k, 4)]
     else:
+        own = own_ref[...]
+        blank = jnp.zeros((192, 64), BF16)
+        keys[0, 0:192, :] = jnp.concatenate([own, blank], axis=1)
+        keys[1, 0:192, :] = pltpu.roll(jnp.concatenate([own, blank], axis=1).astype(F32), 64, 1).astype(BF16)
+        causal = jnp.where(iota((192, 192), 0) <= iota((192, 192), 1), 0.0, -1e30)
         for c in range(4):
-            own_scores(c)
+            own_scores(c, causal)
         keys[0, 192:448, :] = trunk_ref[...]
     keys[1, 192:448, :] = pltpu.roll(keys[0, 192:448, :].astype(F32), 64, 1).astype(BF16)
     live = jnp.where(iota((256, 1), 0) % 32 < cnt_ref[leaf], 0.0, -1e30)
@@ -300,65 +309,85 @@
         odd = dot(ds[2 * u + 1], keys[1], 0, 0) * SCALE
         for n in range(4):
             r = slice(192 * n, 192 * n + 192)
-            at = 4608 * u + 1152 * n
-            dq_ref[:, at:at + 512] = even[r, 0:512].astype(BF16)
-            dq_ref[:, at + 512:at + 640] = (even[r, 512:640] + odd[r, 0:128]).astype(BF16)
-            dq_ref[:, at + 640:at + 1152] = odd[r, 128:640].astype(BF16)
-
-    if comm:
-        for c in range(3):
-            own_keys(c)
+            at = 1152 * n
+            dq_out[u, :, at:at + 512] = even[r, 0:512].astype(BF16)
+            dq_out[u, :, at + 512:at + 640] = (even[r, 512:640] + odd[r, 0:128]).astype(BF16)
+            dq_out[u, :, at + 640:at + 1152] = odd[r, 128:640].astype(BF16)
+        copy = pltpu.make_async_copy(dq_out.at[u], dq_ref.at[:, pl.ds(4608 * u, 4608)], store_sem.at[u])
+        copy.start()
+        return copy
+
+    for c in range(4):
+        own_keys(c)
+    own_done()
+    if comm:
         ring_pass(far_copies, far_value, r_far, m_far, far_send, far_recv)
-        own_keys(3)
-        own_done()
         own_copies = ring_start(lambda k, half: x_own.at[own_at(k, half)], r_own, own_send, own_recv)
+        stores = [d_query(0)]
         sums = ring_sum(far_copies, far_value, r_far)
         rows = dot(spread, jnp.concatenate(sums, axis=0).astype(BF16), 0, 0)
         for d in range(2 * LEAF):
             t_out[d] = rows[2 * d:2 * d + 2].astype(BF16)
 
-        def far_first(j):
-            return lax.rem(j + 24, 2 * LEAF - 1) + 1
-
-        def send_rows(j, c):
-            k = far_first(j)
-            to = lax.rem(me + k, 2 * LEAF)
-            remote(t_out.at[to], t_got.at[me], t_send.at[k], t_recv.at[me], plane(to)).start()
-            return c
-
-        lax.fori_loop(0, 2 * LEAF - 1, send_rows, 0)
+        def row_across(k):
+            to = there + k
+            return remote(t_out.at[to], t_got.at[me], t_send.at[k], t_recv.at[me], {"leaf": k, "head": across})
+
+        def row_here(k):
+            to = lax.rem(leaf + k, LEAF)
+            return remote(t_out.at[here + to], t_got.at[me], t_send.at[LEAF + k], t_recv.at[me], {"leaf": to})
+
+        def send_across(k, c):
+            row_across(k).start()
+            return c
+
+        def send_here(k, c):
+            row_here(k).start()
+            return c
+
+        lax.fori_loop(0, LEAF, send_across, 0)
+        lax.fori_loop(1, LEAF, send_here, 0)
         mine = pltpu.make_async_copy(t_out.at[me], t_got.at[me], t_recv.at[me])
         mine.start()
-        d_query(0)
         ring_pass(own_copies, own_value, r_own, m_own, own_send, own_recv)
-        d_query(1)
+        stores.append(d_query(1))
         sums = ring_sum(own_copies, own_value, r_own)
         for half in range(2):
             pair[half] = sums[half]
-        pair_out = remote(pair.at[1 - deep], pair_in, pair_sem.at[0], pair_sem.at[1], {"head": (1 - deep) * 4 + y})
+        pair_out = remote(pair.at[1 - deep], pair_in, pair_sem.at[0], pair_sem.at[1], {"head": across})
         pair_out.start()
         mine.wait()
 
-        def receive_rows(k, c):
-            source = lax.rem(me + k, 2 * LEAF)
-            remote(t_out.at[source], t_got.at[source], t_send.at[k], t_recv.at[source], plane(source)).wait()
-            return c
-
-        lax.fori_loop(1, 2 * LEAF, receive_rows, 0)
+        def receive_across(k, c):
+            source = there + k
+            row = remote(
+                t_out.at[source], t_got.at[source], t_send.at[k], t_recv.at[source], {"leaf": k, "head": across}
+            )
+            row.wait()
+            return c
+
+        def receive_here(k, c):
+            source = lax.rem(leaf + k, LEAF)
+            at = here + source
+            remote(t_out.at[at], t_got.at[at], t_send.at[LEAF + k], t_recv.at[at], {"leaf": source}).wait()
+            return c
+
+        lax.fori_loop(0, LEAF, receive_across, 0)
+        lax.fori_loop(1, LEAF, receive_here, 0)
         for d in range(2 * LEAF):
             spare_ref[2 * d:2 * d + 2, :] = t_got[d].astype(F32)
+        for copy in ring + far_copies + own_copies:
+            copy.wait_send()
+        for copy in stores:
+            copy.wait()
         pair_out.wait()
         branch_ref[...] = pair[deep] + pair_in[...]
-        for copy in ring + far_copies + own_copies:
-            copy.wait_send()
     else:
-        for c in range(4):
-            own_keys(c)
-        own_done()
-        d_query(0)
-        d_query(1)
+        stores = [d_query(0), d_query(1)]
         spare_ref[...] = x_far[...]
         branch_ref[...] = x_own[...]
+        for copy in stores:
+            copy.wait()
 
 
 def fused_call(comm, ancestors, count, own, trunk, q, do):
@@ -372,7 +401,7 @@
         functools.partial(fused, comm),
         out_shape=(pltpu.VMEM((192, 9216), BF16),) + small + (pltpu.VMEM((128, 128), F32),),
         in_specs=[hbm] * 6,
-        out_specs=(vmem,) * 4,
+        out_specs=(pl.BlockSpec(memory_space=pl.ANY),) + (vmem,) * 3,
         scratch_shapes=[
             pltpu.VMEM((LEAF, LEAF), jnp.int32),
             pltpu.SMEM(count.shape, jnp.int32),
@@ -388,6 +417,7 @@
             pltpu.VMEM((4, 448, 768), BF16),
             pltpu.VMEM((2, 448, WIDE), F32),
             pltpu.VMEM((448, 512), F32),
+            pltpu.VMEM((2, 192, 4608), BF16),
             pltpu.VMEM((LEAF, 4, WIDE), BF16),
             pltpu.VMEM((LEAF, 4, WIDE), BF16),
             pltpu.VMEM((128, WIDE), F32),
@@ -402,7 +432,7 @@
             pltpu.VMEM((24, WIDE), F32),
             pltpu.VMEM((2 * LEAF, 2, WIDE), BF16),
             pltpu.VMEM((2 * LEAF, 2, WIDE), BF16),
-            dma((32,)), dma((LEAF,)), dma((LEAF,)), dma((6,)), dma((6,)), dma((6,)), dma((6,)),
+            dma((32,)), dma((2,)), dma((LEAF,)), dma((LEAF,)), dma((6,)), dma((6,)), dma((6,)), dma((6,)),
             dma((6,)), dma((6,)), dma((2,)), dma((2 * LEAF,)), dma((2 * LEAF,)),
         ],
         compiler_params=pltpu.CompilerParams(
@@ -412,22 +442,24 @@
     )(ancestors, count, own, trunk, q, do)
 
 
-def finish(grad_ref, rows_ref, sum_ref, collect_ref, dq_hbm, branch_ref, trunk_ref, sem):
-    copies = []
-    for k in range(4):
-        part = pl.ds(48 * k, 48)
-        copies.append(pltpu.make_async_copy(grad_ref.at[part], dq_hbm.at[part], sem.at[k]))
-        copies[k].start()
-    branch_ref[...] = sum_ref[:, 0:576]
+def finish(grad_ref, rows_ref, sum_ref, collect_ref, dq_hbm, branch_hbm, trunk_hbm, branch, trunk, sem):
+    copies = [
+        pltpu.make_async_copy(grad_ref, dq_hbm, sem.at[0]),
+        pltpu.make_async_copy(branch, branch_hbm, sem.at[1]),
+        pltpu.make_async_copy(trunk, trunk_hbm, sem.at[2]),
+    ]
+    copies[0].start()
+    branch[...] = sum_ref[:, 0:576]
+    copies[1].start()
     total = dot(collect_ref[...].astype(BF16), rows_ref[...].astype(BF16), 0, 0)
     for b in range(16):
-        trunk_ref[b] = total[b:b + 1, 0:576]
+        trunk[b] = total[b:b + 1, 0:576]
+    copies[2].start()
     for copy in copies:
         copy.wait()
 
 
 def finish_call(grad, rows, total, collect):
-    vmem, hbm = pl.BlockSpec(memory_space=pltpu.VMEM), pl.BlockSpec(memory_space=pl.ANY)
     return pl.pallas_call(
         finish,
         out_shape=(
@@ -435,15 +467,20 @@
             jax.ShapeDtypeStruct((24, 576), F32),
             jax.ShapeDtypeStruct((16, 1, 576), F32),
         ),
-        in_specs=[vmem] * 4,
-        out_specs=(hbm, vmem, vmem),
-        scratch_shapes=[pltpu.SemaphoreType.DMA((4,))],
+        in_specs=[pl.BlockSpec(memory_space=pltpu.VMEM)] * 4,
+        out_specs=(pl.BlockSpec(memory_space=pltpu.HBM),) * 3,
+        scratch_shapes=[
+            pltpu.VMEM((24, 576), F32),
+            pltpu.VMEM((16, 1, 576), F32),
+            pltpu.SemaphoreType.DMA((3,)),
+        ],
         compiler_params=pltpu.CompilerParams(vmem_limit_bytes=16 * 2**20),
         name="finish",
     )(grad, rows, total, collect)
 
 
 def local(queries, d_out, branch_latent, trunk_latent, ancestors, anc_count):
+    ancestors, anc_count = (pltpu.with_memory_space_constraint(a, pltpu.HBM) for a in (ancestors, anc_count))
     grad, total, rows, collect = fused_call(True, ancestors, anc_count, branch_latent, trunk_latent, queries, d_out)
     return finish_call(grad, rows, total, collect)
 

time: 55.9 us -> 51 us (0.912)
  Pallas kernels: 53.7 us -> 50.3 us
  local copies, waits for them, and re-layouts: 1.37 us -> 0 us
    pallas_call x1, Pallas kernels: 51.2 us -> 48.5 us  [fused_call(): pl.pallas_call(functools.partial(fused, comm), out_shape=(pltpu.VMEM((192...]
    unnamed x4 -> x0, local copies, waits for them, and re-layouts: 1.37 us -> none
    pallas_call x1, Pallas kernels: 2.48 us -> 1.83 us  [finish_call(): pl.pallas_call(finish, out_shape=(jax.ShapeDtypeStruct((192, 9216), BF16)...]
where the time goes in v4:
time: 51 us; the launch traced here: 50.9 us
  Pallas kernels  50.3 us (99%)
  between operations  0.64 us (1%)
    pallas_call x1, Pallas kernels, fused_call(): pl.pallas_call(functools.partial(fused, comm), out_shape=(pltpu.VMEM((192...  48.5 us
    pallas_call x1, Pallas kernels, finish_call(): pl.pallas_call(finish, out_shape=(jax.ShapeDtypeStruct((192, 9216), BF16)...  1.83 us

profile of v4, /device:TPU:6, one launch (start us, length us, event | category | flops | bytes accessed | tf_op | source)
XLA Modules:
  0.0 50.9 jit_solution(2189941078987264677)
XLA Ops:
  0.6 48.5 %backward.1 = (bf16[192,9216]{1,0:T(8,128)(2,1)S(1)}, f32[24,640]{1,0:T(8,128)S(1)}, f32[128,640]{1,0:T(8,128)S(1)}, f32[128,128]{1,0:T(8,128)S(1)}) custom-call(s32[32,32]{1,0:T(8,128)} %anc_hbm.1, s32[32]{0:T(128)} %cnt_hbm.1, bf16[192,576]{1,0:T(8,128)(2,1)} %own_hbm.1, bf16[16,8,576]{2,1,0:T(8,128)(2,1)} %trunk_hbm.1, bf16[192,9216]{1,0:T(8,128)(2,1)} %q_hbm.1, ...), custom_call_target="tpu_custom_call" | custom-call | tf_op jit(solution)/shard_map/backward/pallas_call | solution.py:400
  49.1 1.8 %finish.1 = (bf16[192,9216]{1,0:T(8,128)(2,1)}, f32[24,576]{1,0:T(8,128)}, f32[16,1,576]{2,1,0:T(1,128)}) custom-call(bf16[192,9216]{1,0:T(8,128)(2,1)S(1)} %get-tuple-element.7.grad_ref, f32[128,640]{1,0:T(8,128)S(1)} %get-tuple-element.8.rows_ref, f32[24,640]{1,0:T(8,128)S(1)} %get-tuple-element.9.sum_ref, f32[128,128]{1,0:T(8,128)S(1)} %get-tuple-element.10.collect_ref), custom_call_target="tpu_custom_call" | custom-call | tf_op jit(solution)/shard_map/finish/pallas_call | solution.py:463

commit v5 on v4

--- a/solution.py
+++ b/solution.py
@@ -56,10 +56,10 @@
 
 def fused(comm, anc_hbm, cnt_hbm, own_hbm, trunk_hbm, q_hbm, do_hbm, dq_ref, branch_ref, spare_ref, collect_ref,
           anc_ref, cnt_ref, own_ref, trunk_ref, small_sem,
-          qs, dos, keys, sown, dpown, p_own, ds, acc_k, acc_v, dq_out,
+          qs, dos, keys, sown, dpown, prob, ds, acc_k, acc_v, dq_out,
           g_out, g_got, g_tall, slabs, x_far, x_own, r_far, r_own, m_far, m_own, pair, pair_in, t_out, t_got,
-          load_sem, store_sem, g_send, g_recv, ring_send, ring_recv, far_send, far_recv, own_send, own_recv,
-          pair_sem, t_send, t_recv):
+          load_sem, store_sem, g_sem, ring_send, ring_recv, far_send, far_recv, own_send, own_recv,
+          pair_sem, t_sem):
     small = [
         pltpu.make_async_copy(anc_hbm, anc_ref, small_sem.at[0]),
         pltpu.make_async_copy(trunk_hbm, trunk_ref, small_sem.at[1]),
@@ -98,18 +98,19 @@
     loads = {}
     for u in range(2):
         for par in range(2):
-            group = []
+            k = 4 * u + 2 * par
             for n in range(4):
                 h = 4 * u + n
                 at = pl.ds(192 * h, 192)
-                k = 16 * u + 8 * par + 2 * n
-                group.append(pltpu.make_async_copy(
-                    q_hbm.at[:, pl.ds(1152 * h + 512 * par, WIDE)], qs.at[par, at], load_sem.at[k]))
-                group.append(pltpu.make_async_copy(
-                    do_hbm.at[:, pl.ds(1024 * h + 512 * par, 512)], dos.at[par, at], load_sem.at[k + 1]))
-            for copy in group:
-                copy.start()
-            loads[u, par] = group
+                pltpu.make_async_copy(
+                    q_hbm.at[:, pl.ds(1152 * h + 512 * par, WIDE)], qs.at[par, at], load_sem.at[k]).start()
+                pltpu.make_async_copy(
+                    do_hbm.at[:, pl.ds(1024 * h + 512 * par, 512)], dos.at[par, at], load_sem.at[k + 1]).start()
+            rows = pl.ds(768 * u, 768)
+            loads[u, par] = [
+                pltpu.make_async_copy(ref.at[par, rows], ref.at[par, rows], load_sem.at[k + n])
+                for n, ref in enumerate((qs, dos))
+            ]
     chunks = [(u, par) for u in range(2) for par in range(2)]
 
     def q_of(u, par):
@@ -135,19 +136,30 @@
             copy.wait()
         u, par = chunks[c]
         s = dot(keys[par, 0:192, :], q_of(u, par), 1, 1)
-        sown[c] = s + jnp.concatenate([causal] * 4, axis=1)
-        dpown[c] = dot(keys[0, 0:192, 0:512], do_of(u, par), 1, 1)
+        sown[c, 0:192, :] = s + jnp.concatenate([causal] * 4, axis=1)
+        dpown[c, 0:192, :] = dot(keys[0, 0:192, 0:512], do_of(u, par), 1, 1)
+
+    def live(n):
+        return jnp.where(iota((n, 1), 0) % 32 < cnt_ref[leaf], 0.0, -1e30)
+
+    def shifted(lo, hi):
+        keys[1, lo:hi, :] = pltpu.roll(keys[0, lo:hi, :].astype(F32), 64, 1).astype(BF16)
+
+    def near_scores(c):
+        u, par = chunks[c]
+        sown[c, 192:384, :] = dot(keys[par, 192:384, :], q_of(u, par), 1, 1) + live(192)
+        dpown[c, 192:384, :] = dot(keys[0, 192:384, 0:512], do_of(u, par), 1, 1)
 
     if comm:
         pl.semaphore_wait(barrier, 2 * LEAF + 1)
 
         def send(k, c):
             to = lax.rem(leaf + k, LEAF)
-            remote(g_out.at[to], g_got.at[leaf], g_send.at[k], g_recv.at[leaf], {"leaf": to}).start()
+            remote(g_out.at[to], g_got.at[leaf], g_sem.at[0], g_sem.at[1], {"leaf": to}).start()
             return c
 
         lax.fori_loop(1, LEAF, send, 0)
-        mine = pltpu.make_async_copy(g_out.at[leaf], g_got.at[leaf], g_recv.at[leaf])
+        mine = pltpu.make_async_copy(g_out.at[leaf], g_got.at[leaf], g_sem.at[1])
         mine.start()
         i = iota((64, 1), 0)
         owner, rank = owner_and_rank(anc_ref[pl.ds(leaf, 1), :], i % 32)
@@ -165,14 +177,9 @@
         causal = jnp.where(iota((192, 192), 0) <= iota((192, 192), 1), 0.0, -1e30)
         for c in range(4):
             own_scores(c, causal)
-        mine.wait()
-
-        def receive(k, c):
-            source = lax.rem(leaf + k, LEAF)
-            remote(g_out.at[source], g_got.at[source], g_send.at[k], g_recv.at[source], {"leaf": source}).wait()
-            return c
-
-        lax.fori_loop(1, LEAF, receive, 0)
+        others = pl.ds(0, LEAF - 1)
+        remote(g_out.at[others], g_got, g_sem.at[0], g_sem.at[1], right).wait_send()
+        remote(g_out, g_got, g_sem.at[0], g_sem.at[1], right).wait_recv()
         for b in range(LEAF):
             g_tall[4 * b:4 * b + 4, :] = g_got[b].astype(F32)
         slabs[y] = dot(take, g_tall[...].astype(BF16), 1, 0).astype(BF16)
@@ -193,10 +200,14 @@
         ring[5].start()
         hop(2, up, 1, right).wait_recv()
         hop(3, down, 0, left).wait_recv()
+        for n, k in enumerate((0, 1, 3)):
+            keys[0, 192 + 64 * n:256 + 64 * n, :] = slabs[lax.rem(y + k, 4)]
+        shifted(192, 384)
+        for c in range(4):
+            near_scores(c)
         hop(4, far, 0, right).wait_recv()
         hop(5, far, 1, left).wait_recv()
-        for k in range(4):
-            keys[0, 192 + 64 * k:256 + 64 * k, :] = slabs[lax.rem(y + k, 4)]
+        keys[0, 384:448, :] = slabs[far]
     else:
         own = own_ref[...]
         blank = jnp.zeros((192, 64), BF16)
@@ -205,34 +216,38 @@
         causal = jnp.where(iota((192, 192), 0) <= iota((192, 192), 1), 0.0, -1e30)
         for c in range(4):
             own_scores(c, causal)
-        keys[0, 192:448, :] = trunk_ref[...]
-    keys[1, 192:448, :] = pltpu.roll(keys[0, 192:448, :].astype(F32), 64, 1).astype(BF16)
-    live = jnp.where(iota((256, 1), 0) % 32 < cnt_ref[leaf], 0.0, -1e30)
-
-    def far_scores(c):
+        keys[0, 192:320, :] = trunk_ref[0:128, :]
+        keys[0, 320:384, :] = trunk_ref[192:256, :]
+        shifted(192, 384)
+        for c in range(4):
+            near_scores(c)
+        keys[0, 384:448, :] = trunk_ref[128:192, :]
+    shifted(384, 448)
+
+    def last_scores(c):
         u, par = chunks[c]
-        return (dot(keys[par, 192:448, :], q_of(u, par), 1, 1) + live,
-                dot(keys[0, 192:448, 0:512], do_of(u, par), 1, 1))
-
-    ahead = far_scores(0)
+        return (dot(keys[par, 384:448, :], q_of(u, par), 1, 1) + live(64),
+                dot(keys[0, 384:448, 0:512], do_of(u, par), 1, 1))
+
+    ahead = last_scores(0)
     for c in range(4):
         u, par = chunks[c]
-        sf, dpf = ahead
+        sl, dpl = ahead
         if c < 3:
-            ahead = far_scores(c + 1)
+            ahead = last_scores(c + 1)
         so, dpo = sown[c], dpown[c]
-        m = jnp.maximum(jnp.max(sf, axis=0, keepdims=True), jnp.max(so, axis=0, keepdims=True))
-        ef = jnp.exp2((sf - m) * (SCALE * LOG2E))
+        m = jnp.maximum(jnp.max(sl, axis=0, keepdims=True), jnp.max(so, axis=0, keepdims=True))
+        el = jnp.exp2((sl - m) * (SCALE * LOG2E))
         eo = jnp.exp2((so - m) * (SCALE * LOG2E))
-        inv = 1.0 / (jnp.sum(ef, axis=0, keepdims=True) + jnp.sum(eo, axis=0, keepdims=True))
-        pf, po = ef * inv, eo * inv
-        delta = jnp.sum(pf * dpf, axis=0, keepdims=True) + jnp.sum(po * dpo, axis=0, keepdims=True)
-        dsf = (pf * (dpf - delta)).astype(BF16)
-        ds[c, 192:448, :] = dsf
-        ds[c, 0:192, :] = (po * (dpo - delta)).astype(BF16)
-        p_own[c] = po.astype(BF16)
-        dk = dot(dsf, q_of(u, par), 1, 0)
-        dv = dot(pf.astype(BF16), do_of(u, par), 1, 0)
+        inv = 1.0 / (jnp.sum(el, axis=0, keepdims=True) + jnp.sum(eo, axis=0, keepdims=True))
+        pb, po = el * inv, eo * inv
+        delta = jnp.sum(pb * dpl, axis=0, keepdims=True) + jnp.sum(po * dpo, axis=0, keepdims=True)
+        ds[c, 0:384, :] = (po * (dpo - delta)).astype(BF16)
+        ds[c, 384:448, :] = (pb * (dpl - delta)).astype(BF16)
+        prob[c, 0:384, :] = po.astype(BF16)
+        prob[c, 384:448, :] = pb.astype(BF16)
+        dk = dot(ds[c, 192:448, :], q_of(u, par), 1, 0)
+        dv = dot(prob[c, 192:448, :], do_of(u, par), 1, 0)
         if u == 0:
             acc_k[par, 192:448, :] = dk
         else:
@@ -246,9 +261,9 @@
         dk = (acc_k[0, lo:lo + n, :] + pltpu.roll(acc_k[1, lo:lo + n, :], 576, 1)) * SCALE
         return jnp.concatenate([dk[:, 0:512] + acc_v[lo:lo + n, :], dk[:, 512:WIDE]], axis=1)
 
-    for k in range(4):
+    for at, k in enumerate((0, 1, 3, 2)):
         for half in range(2):
-            x_far[k, half] = merged(192 + 64 * k + 32 * half, 32).astype(BF16)
+            x_far[k, half] = merged(192 + 64 * at + 32 * half, 32).astype(BF16)
 
     def ring_start(x, mid, send_sem, recv_sem):
         copies = [
@@ -281,7 +296,7 @@
     def own_keys(c):
         u, par = chunks[c]
         dk = dot(ds[c, 0:192, :], q_of(u, par), 1, 0)
-        dv = dot(p_own[c], do_of(u, par), 1, 0)
+        dv = dot(prob[c, 0:192, :], do_of(u, par), 1, 0)
         if u == 0:
             acc_k[par, 0:192, :] = dk
         else:
@@ -326,16 +341,17 @@
         stores = [d_query(0)]
         sums = ring_sum(far_copies, far_value, r_far)
         rows = dot(spread, jnp.concatenate(sums, axis=0).astype(BF16), 0, 0)
+        ring_pass(own_copies, own_value, r_own, m_own, own_send, own_recv)
         for d in range(2 * LEAF):
             t_out[d] = rows[2 * d:2 * d + 2].astype(BF16)
 
         def row_across(k):
             to = there + k
-            return remote(t_out.at[to], t_got.at[me], t_send.at[k], t_recv.at[me], {"leaf": k, "head": across})
+            return remote(t_out.at[to], t_got.at[me], t_sem.at[0], t_sem.at[1], {"leaf": k, "head": across})
 
         def row_here(k):
             to = lax.rem(leaf + k, LEAF)
-            return remote(t_out.at[here + to], t_got.at[me], t_send.at[LEAF + k], t_recv.at[me], {"leaf": to})
+            return remote(t_out.at[here + to], t_got.at[me], t_sem.at[0], t_sem.at[1], {"leaf": to})
 
         def send_across(k, c):
             row_across(k).start()
@@ -347,33 +363,17 @@
 
         lax.fori_loop(0, LEAF, send_across, 0)
         lax.fori_loop(1, LEAF, send_here, 0)
-        mine = pltpu.make_async_copy(t_out.at[me], t_got.at[me], t_recv.at[me])
+        mine = pltpu.make_async_copy(t_out.at[me], t_got.at[me], t_sem.at[1])
         mine.start()
-        ring_pass(own_copies, own_value, r_own, m_own, own_send, own_recv)
         stores.append(d_query(1))
         sums = ring_sum(own_copies, own_value, r_own)
         for half in range(2):
             pair[half] = sums[half]
         pair_out = remote(pair.at[1 - deep], pair_in, pair_sem.at[0], pair_sem.at[1], {"head": across})
         pair_out.start()
-        mine.wait()
-
-        def receive_across(k, c):
-            source = there + k
-            row = remote(
-                t_out.at[source], t_got.at[source], t_send.at[k], t_recv.at[source], {"leaf": k, "head": across}
-            )
-            row.wait()
-            return c
-
-        def receive_here(k, c):
-            source = lax.rem(leaf + k, LEAF)
-            at = here + source
-            remote(t_out.at[at], t_got.at[at], t_send.at[LEAF + k], t_recv.at[at], {"leaf": source}).wait()
-            return c
-
-        lax.fori_loop(0, LEAF, receive_across, 0)
-        lax.fori_loop(1, LEAF, receive_here, 0)
+        others = pl.ds(0, 2 * LEAF - 1)
+        remote(t_out.at[others], t_got, t_sem.at[0], t_sem.at[1], right).wait_send()
+        remote(t_out, t_got, t_sem.at[0], t_sem.at[1], right).wait_recv()
         for d in range(2 * LEAF):
             spare_ref[2 * d:2 * d + 2, :] = t_got[d].astype(F32)
         for copy in ring + far_copies + own_copies:
@@ -411,9 +411,9 @@
             pltpu.VMEM((2, 1536, WIDE), BF16),
             pltpu.VMEM((2, 1536, 512), BF16),
             pltpu.VMEM((2, 448, WIDE), BF16),
-            pltpu.VMEM((4, 192, 768), F32),
-            pltpu.VMEM((4, 192, 768), F32),
-            pltpu.VMEM((4, 192, 768), BF16),
+            pltpu.VMEM((4, 384, 768), F32),
+            pltpu.VMEM((4, 384, 768), F32),
+            pltpu.VMEM((4, 448, 768), BF16),
             pltpu.VMEM((4, 448, 768), BF16),
             pltpu.VMEM((2, 448, WIDE), F32),
             pltpu.VMEM((448, 512), F32),
@@ -432,8 +432,8 @@
             pltpu.VMEM((24, WIDE), F32),
             pltpu.VMEM((2 * LEAF, 2, WIDE), BF16),
             pltpu.VMEM((2 * LEAF, 2, WIDE), BF16),
-            dma((32,)), dma((2,)), dma((LEAF,)), dma((LEAF,)), dma((6,)), dma((6,)), dma((6,)), dma((6,)),
-            dma((6,)), dma((6,)), dma((2,)), dma((2 * LEAF,)), dma((2 * LEAF,)),
+            dma((8,)), dma((2,)), dma((2,)), dma((6,)), dma((6,)), dma((6,)), dma((6,)), dma((6,)), dma((6,)),
+            dma((2,)), dma((2,)),
         ],
         compiler_params=pltpu.CompilerParams(
             collective_id=0, has_side_effects=True, vmem_limit_bytes=VMEM_LIMIT

time: 51 us -> 48.1 us (0.943)
  Pallas kernels: 50.3 us -> 47.2 us
    pallas_call x1, Pallas kernels: 48.5 us -> 45.4 us  [fused_call(): pl.pallas_call(functools.partial(fused, comm), out_shape=(pltpu.VMEM((192...]
where the time goes in v5:
time: 48.1 us; the launch traced here: 47.9 us
  Pallas kernels  47.2 us (98%)
  between operations  0.64 us (1%)
    pallas_call x1, Pallas kernels, fused_call(): pl.pallas_call(functools.partial(fused, comm), out_shape=(pltpu.VMEM((192...  45.4 us
    pallas_call x1, Pallas kernels, finish_call(): pl.pallas_call(finish, out_shape=(jax.ShapeDtypeStruct((192, 9216), BF16)...  1.83 us

profile of v5, /device:TPU:6, one launch (start us, length us, event | category | flops | bytes accessed | tf_op | source)
XLA Modules:
  0.0 47.9 jit_solution(10068813012113372197)
XLA Ops:
  0.6 45.4 %backward.1 = (bf16[192,9216]{1,0:T(8,128)(2,1)S(1)}, f32[24,640]{1,0:T(8,128)S(1)}, f32[128,640]{1,0:T(8,128)S(1)}, f32[128,128]{1,0:T(8,128)S(1)}) custom-call(s32[32,32]{1,0:T(8,128)} %anc_hbm.1, s32[32]{0:T(128)} %cnt_hbm.1, bf16[192,576]{1,0:T(8,128)(2,1)} %own_hbm.1, bf16[16,8,576]{2,1,0:T(8,128)(2,1)} %trunk_hbm.1, bf16[192,9216]{1,0:T(8,128)(2,1)} %q_hbm.1, ...), custom_call_target="tpu_custom_call" | custom-call | tf_op jit(solution)/shard_map/backward/pallas_call | solution.py:400
  46.0 1.8 %finish.1 = (bf16[192,9216]{1,0:T(8,128)(2,1)}, f32[24,576]{1,0:T(8,128)}, f32[16,1,576]{2,1,0:T(1,128)}) custom-call(bf16[192,9216]{1,0:T(8,128)(2,1)S(1)} %get-tuple-element.7.grad_ref, f32[128,640]{1,0:T(8,128)S(1)} %get-tuple-element.8.rows_ref, f32[24,640]{1,0:T(8,128)S(1)} %get-tuple-element.9.sum_ref, f32[128,128]{1,0:T(8,128)S(1)} %get-tuple-element.10.collect_ref), custom_call_target="tpu_custom_call" | custom-call | tf_op jit(solution)/shard_map/finish/pallas_call | solution.py:463

commit v6 on v5

--- a/solution.py
+++ b/solution.py
@@ -56,7 +56,7 @@
 
 def fused(comm, anc_hbm, cnt_hbm, own_hbm, trunk_hbm, q_hbm, do_hbm, dq_ref, branch_ref, spare_ref, collect_ref,
           anc_ref, cnt_ref, own_ref, trunk_ref, small_sem,
-          qs, dos, keys, sown, dpown, prob, ds, acc_k, acc_v, dq_out,
+          qs, dos, keys, eown, dpown, stats, prob, ds, acc_k, acc_v, dq_out,
           g_out, g_got, g_tall, slabs, x_far, x_own, r_far, r_own, m_far, m_own, pair, pair_in, t_out, t_got,
           load_sem, store_sem, g_sem, ring_send, ring_recv, far_send, far_recv, own_send, own_recv,
           pair_sem, t_sem):
@@ -75,21 +75,29 @@
         right = {"head": deep * 4 + lax.rem(y + 1, 4)}
         left = {"head": deep * 4 + lax.rem(y + 3, 4)}
 
-        here, there = deep * LEAF, (1 - deep) * LEAF
-        across = (1 - deep) * 4 + y
+        z, seat = leaf // 8, lax.rem(leaf, 8)
+        across = {"head": (1 - deep) * 4 + y}
+
+        def each_seat(visit, index, where, first=0):
+            def step(k, c):
+                at = lax.rem(seat + k, 8) if first else k
+                visit(index + at, where(at))
+                return c
+
+            lax.fori_loop(first, 8, step, 0)
+
+        def plane_peers(visit):
+            for r in (4, 3, 5, 2, 6, 1, 7, 0):
+                place = lax.rem(deep * 4 + z + r, 8)
+                column, base = (place // 4) * 4 + y, lax.rem(place, 4) * 8
+                each_seat(visit, place * 8, lambda at: {"leaf": base + at, "head": column}, int(r == 0))
+
+        def leaf_peers(visit):
+            for other in (3 - 3 * (z // 2), 2 - z // 2, z + 1 - 2 * lax.rem(z, 2), z):
+                each_seat(visit, other * 8, lambda at: {"leaf": other * 8 + at}, int(other is z))
 
         barrier = pltpu.get_barrier_semaphore()
-
-        def greet_across(k, c):
-            signal(barrier, {"leaf": k, "head": across})
-            return c
-
-        def greet(k, c):
-            signal(barrier, {"leaf": lax.rem(leaf + k, LEAF)})
-            return c
-
-        lax.fori_loop(0, LEAF, greet_across, 0)
-        lax.fori_loop(1, LEAF, greet, 0)
+        plane_peers(lambda index, where: signal(barrier, where))
         signal(barrier, left)
         signal(barrier, right)
     else:
@@ -135,9 +143,17 @@
         for copy in loads[chunks[c]]:
             copy.wait()
         u, par = chunks[c]
-        s = dot(keys[par, 0:192, :], q_of(u, par), 1, 1)
-        sown[c, 0:192, :] = s + jnp.concatenate([causal] * 4, axis=1)
-        dpown[c, 0:192, :] = dot(keys[0, 0:192, 0:512], do_of(u, par), 1, 1)
+        s = dot(keys[par, 0:192, :], q_of(u, par), 1, 1) + jnp.concatenate([causal] * 4, axis=1)
+        keep(c, 0, s, dot(keys[0, 0:192, 0:512], do_of(u, par), 1, 1))
+
+    def keep(c, part, s, dp):
+        lo, top = 192 * part, jnp.max(s, axis=0, keepdims=True)
+        e = jnp.exp2((s - top) * (SCALE * LOG2E))
+        eown[c, lo:lo + 192, :] = e
+        dpown[c, lo:lo + 192, :] = dp
+        stats[c, 3 * part:3 * part + 1, :] = top
+        stats[c, 3 * part + 1:3 * part + 2, :] = jnp.sum(e, axis=0, keepdims=True)
+        stats[c, 3 * part + 2:3 * part + 3, :] = jnp.sum(e * dp, axis=0, keepdims=True)
 
     def live(n):
         return jnp.where(iota((n, 1), 0) % 32 < cnt_ref[leaf], 0.0, -1e30)
@@ -147,18 +163,13 @@
 
     def near_scores(c):
         u, par = chunks[c]
-        sown[c, 192:384, :] = dot(keys[par, 192:384, :], q_of(u, par), 1, 1) + live(192)
-        dpown[c, 192:384, :] = dot(keys[0, 192:384, 0:512], do_of(u, par), 1, 1)
+        s = dot(keys[par, 192:384, :], q_of(u, par), 1, 1) + live(192)
+        keep(c, 1, s, dot(keys[0, 192:384, 0:512], do_of(u, par), 1, 1))
 
     if comm:
         pl.semaphore_wait(barrier, 2 * LEAF + 1)
 
-        def send(k, c):
-            to = lax.rem(leaf + k, LEAF)
-            remote(g_out.at[to], g_got.at[leaf], g_sem.at[0], g_sem.at[1], {"leaf": to}).start()
-            return c
-
-        lax.fori_loop(1, LEAF, send, 0)
+        leaf_peers(lambda to, where: remote(g_out.at[to], g_got.at[leaf], g_sem.at[0], g_sem.at[1], where).start())
         mine = pltpu.make_async_copy(g_out.at[leaf], g_got.at[leaf], g_sem.at[1])
         mine.start()
         i = iota((64, 1), 0)
@@ -235,17 +246,24 @@
         sl, dpl = ahead
         if c < 3:
             ahead = last_scores(c + 1)
-        so, dpo = sown[c], dpown[c]
-        m = jnp.maximum(jnp.max(sl, axis=0, keepdims=True), jnp.max(so, axis=0, keepdims=True))
+        tops = [stats[c, 3 * part:3 * part + 1, :] for part in range(2)]
+        m = jnp.maximum(jnp.maximum(tops[0], tops[1]), jnp.max(sl, axis=0, keepdims=True))
         el = jnp.exp2((sl - m) * (SCALE * LOG2E))
-        eo = jnp.exp2((so - m) * (SCALE * LOG2E))
-        inv = 1.0 / (jnp.sum(el, axis=0, keepdims=True) + jnp.sum(eo, axis=0, keepdims=True))
-        pb, po = el * inv, eo * inv
-        delta = jnp.sum(pb * dpl, axis=0, keepdims=True) + jnp.sum(po * dpo, axis=0, keepdims=True)
-        ds[c, 0:384, :] = (po * (dpo - delta)).astype(BF16)
+        total, delta = jnp.sum(el, axis=0, keepdims=True), jnp.sum(el * dpl, axis=0, keepdims=True)
+        factor = [jnp.exp2((top - m) * (SCALE * LOG2E)) for top in tops]
+        for part in range(2):
+            total = total + factor[part] * stats[c, 3 * part + 1:3 * part + 2, :]
+            delta = delta + factor[part] * stats[c, 3 * part + 2:3 * part + 3, :]
+        inv = 1.0 / total
+        delta = delta * inv
+        for part in range(2):
+            rows = slice(192 * part, 192 * part + 192)
+            pb = eown[c, rows, :] * (factor[part] * inv)
+            prob[c, rows, :] = pb.astype(BF16)
+            ds[c, rows, :] = (pb * (dpown[c, rows, :] - delta)).astype(BF16)
+        pb = el * inv
+        prob[c, 384:448, :] = pb.astype(BF16)
         ds[c, 384:448, :] = (pb * (dpl - delta)).astype(BF16)
-        prob[c, 0:384, :] = po.astype(BF16)
-        prob[c, 384:448, :] = pb.astype(BF16)
         dk = dot(ds[c, 192:448, :], q_of(u, par), 1, 0)
         dv = dot(prob[c, 192:448, :], do_of(u, par), 1, 0)
         if u == 0:
@@ -341,35 +359,18 @@
         stores = [d_query(0)]
         sums = ring_sum(far_copies, far_value, r_far)
         rows = dot(spread, jnp.concatenate(sums, axis=0).astype(BF16), 0, 0)
-        ring_pass(own_copies, own_value, r_own, m_own, own_send, own_recv)
         for d in range(2 * LEAF):
             t_out[d] = rows[2 * d:2 * d + 2].astype(BF16)
 
-        def row_across(k):
-            to = there + k
-            return remote(t_out.at[to], t_got.at[me], t_sem.at[0], t_sem.at[1], {"leaf": k, "head": across})
-
-        def row_here(k):
-            to = lax.rem(leaf + k, LEAF)
-            return remote(t_out.at[here + to], t_got.at[me], t_sem.at[0], t_sem.at[1], {"leaf": to})
-
-        def send_across(k, c):
-            row_across(k).start()
-            return c
-
-        def send_here(k, c):
-            row_here(k).start()
-            return c
-
-        lax.fori_loop(0, LEAF, send_across, 0)
-        lax.fori_loop(1, LEAF, send_here, 0)
+        plane_peers(lambda to, where: remote(t_out.at[to], t_got.at[me], t_sem.at[0], t_sem.at[1], where).start())
         mine = pltpu.make_async_copy(t_out.at[me], t_got.at[me], t_sem.at[1])
         mine.start()
+        ring_pass(own_copies, own_value, r_own, m_own, own_send, own_recv)
         stores.append(d_query(1))
         sums = ring_sum(own_copies, own_value, r_own)
         for half in range(2):
-            pair[half] = sums[half]
-        pair_out = remote(pair.at[1 - deep], pair_in, pair_sem.at[0], pair_sem.at[1], {"head": across})
+            pair[half] = sums[half].astype(BF16)
+        pair_out = remote(pair.at[1 - deep], pair_in, pair_sem.at[0], pair_sem.at[1], across)
         pair_out.start()
         others = pl.ds(0, 2 * LEAF - 1)
         remote(t_out.at[others], t_got, t_sem.at[0], t_sem.at[1], right).wait_send()
@@ -381,7 +382,8 @@
         for copy in stores:
             copy.wait()
         pair_out.wait()
-        branch_ref[...] = pair[deep] + pair_in[...]
+        kept = jnp.where(deep == 0, sums[0], sums[1])
+        branch_ref[...] = kept + pair_in[...].astype(F32)
     else:
         stores = [d_query(0), d_query(1)]
         spare_ref[...] = x_far[...]
@@ -413,6 +415,7 @@
             pltpu.VMEM((2, 448, WIDE), BF16),
             pltpu.VMEM((4, 384, 768), F32),
             pltpu.VMEM((4, 384, 768), F32),
+            pltpu.VMEM((4, 8, 768), F32),
             pltpu.VMEM((4, 448, 768), BF16),
             pltpu.VMEM((4, 448, 768), BF16),
             pltpu.VMEM((2, 448, WIDE), F32),
@@ -428,8 +431,8 @@
             pltpu.VMEM((6, 24, WIDE), BF16),
             pltpu.VMEM((2, 32, WIDE), BF16),
             pltpu.VMEM((2, 24, WIDE), BF16),
-            pltpu.VMEM((2, 24, WIDE), F32),
-            pltpu.VMEM((24, WIDE), F32),
+            pltpu.VMEM((2, 24, WIDE), BF16),
+            pltpu.VMEM((24, WIDE), BF16),
             pltpu.VMEM((2 * LEAF, 2, WIDE), BF16),
             pltpu.VMEM((2 * LEAF, 2, WIDE), BF16),
             dma((8,)), dma((2,)), dma((2,)), dma((6,)), dma((6,)), dma((6,)), dma((6,)), dma((6,)), dma((6,)),

time: 48.1 us -> 47.9 us (level)
  no operation moved by 1% of the time
where the time goes in v6:
time: 47.9 us; the launch traced here: 47.8 us
  Pallas kernels  47.1 us (98%)
  between operations  0.64 us (1%)
    pallas_call x1, Pallas kernels, fused_call(): pl.pallas_call(functools.partial(fused, comm), out_shape=(pltpu.VMEM((192...  45.3 us
    pallas_call x1, Pallas kernels, finish_call(): pl.pallas_call(finish, out_shape=(jax.ShapeDtypeStruct((192, 9216), BF16)...  1.83 us

profile of v6, /device:TPU:6, one launch (start us, length us, event | category | flops | bytes accessed | tf_op | source)
XLA Modules:
  0.0 47.8 jit_solution(14073316670883671896)
XLA Ops:
  0.6 45.3 %backward.1 = (bf16[192,9216]{1,0:T(8,128)(2,1)S(1)}, f32[24,640]{1,0:T(8,128)S(1)}, f32[128,640]{1,0:T(8,128)S(1)}, f32[128,128]{1,0:T(8,128)S(1)}) custom-call(s32[32,32]{1,0:T(8,128)} %anc_hbm.1, s32[32]{0:T(128)} %cnt_hbm.1, bf16[192,576]{1,0:T(8,128)(2,1)} %own_hbm.1, bf16[16,8,576]{2,1,0:T(8,128)(2,1)} %trunk_hbm.1, bf16[192,9216]{1,0:T(8,128)(2,1)} %q_hbm.1, ...), custom_call_target="tpu_custom_call" | custom-call | tf_op jit(solution)/shard_map/backward/pallas_call | solution.py:402
  45.9 1.8 %finish.1 = (bf16[192,9216]{1,0:T(8,128)(2,1)}, f32[24,576]{1,0:T(8,128)}, f32[16,1,576]{2,1,0:T(1,128)}) custom-call(bf16[192,9216]{1,0:T(8,128)(2,1)S(1)} %get-tuple-element.7.grad_ref, f32[128,640]{1,0:T(8,128)S(1)} %get-tuple-element.8.rows_ref, f32[24,640]{1,0:T(8,128)S(1)} %get-tuple-element.9.sum_ref, f32[128,128]{1,0:T(8,128)S(1)} %get-tuple-element.10.collect_ref), custom_call_target="tpu_custom_call" | custom-call | tf_op jit(solution)/shard_map/finish/pallas_call | solution.py:466

commit v7 on v6

--- a/solution.py
+++ b/solution.py
@@ -354,9 +354,10 @@
         own_keys(c)
     own_done()
     if comm:
+        own_copies = ring_start(lambda k, half: x_own.at[own_at(k, half)], r_own, own_send, own_recv)
         ring_pass(far_copies, far_value, r_far, m_far, far_send, far_recv)
-        own_copies = ring_start(lambda k, half: x_own.at[own_at(k, half)], r_own, own_send, own_recv)
         stores = [d_query(0)]
+        ring_pass(own_copies, own_value, r_own, m_own, own_send, own_recv)
         sums = ring_sum(far_copies, far_value, r_far)
         rows = dot(spread, jnp.concatenate(sums, axis=0).astype(BF16), 0, 0)
         for d in range(2 * LEAF):
@@ -365,13 +366,12 @@
         plane_peers(lambda to, where: remote(t_out.at[to], t_got.at[me], t_sem.at[0], t_sem.at[1], where).start())
         mine = pltpu.make_async_copy(t_out.at[me], t_got.at[me], t_sem.at[1])
         mine.start()
-        ring_pass(own_copies, own_value, r_own, m_own, own_send, own_recv)
-        stores.append(d_query(1))
         sums = ring_sum(own_copies, own_value, r_own)
         for half in range(2):
             pair[half] = sums[half].astype(BF16)
         pair_out = remote(pair.at[1 - deep], pair_in, pair_sem.at[0], pair_sem.at[1], across)
         pair_out.start()
+        stores.append(d_query(1))
         others = pl.ds(0, 2 * LEAF - 1)
         remote(t_out.at[others], t_got, t_sem.at[0], t_sem.at[1], right).wait_send()
         remote(t_out, t_got, t_sem.at[0], t_sem.at[1], right).wait_recv()

time: 47.9 us -> 46.6 us (0.973)
  the two profiles are of different devices: /device:TPU:6 before, /device:TPU:1 now
where the time goes in v7:
time: 46.6 us; the launch traced here: 46.5 us
  Pallas kernels  45.9 us (98%)
  between operations  0.64 us (1%)
    pallas_call x1, Pallas kernels, fused_call(): pl.pallas_call(functools.partial(fused, comm), out_shape=(pltpu.VMEM((192...  44 us
    pallas_call x1, Pallas kernels, finish_call(): pl.pallas_call(finish, out_shape=(jax.ShapeDtypeStruct((192, 9216), BF16)...  1.83 us

profile of v7, /device:TPU:1, one launch (start us, length us, event | category | flops | bytes accessed | tf_op | source)
XLA Modules:
  0.0 46.5 jit_solution(9524005338769296973)
XLA Ops:
  0.6 44.0 %backward.1 = (bf16[192,9216]{1,0:T(8,128)(2,1)S(1)}, f32[24,640]{1,0:T(8,128)S(1)}, f32[128,640]{1,0:T(8,128)S(1)}, f32[128,128]{1,0:T(8,128)S(1)}) custom-call(s32[32,32]{1,0:T(8,128)} %anc_hbm.1, s32[32]{0:T(128)} %cnt_hbm.1, bf16[192,576]{1,0:T(8,128)(2,1)} %own_hbm.1, bf16[16,8,576]{2,1,0:T(8,128)(2,1)} %trunk_hbm.1, bf16[192,9216]{1,0:T(8,128)(2,1)} %q_hbm.1, ...), custom_call_target="tpu_custom_call" | custom-call | tf_op jit(solution)/shard_map/backward/pallas_call | solution.py:402
  44.7 1.8 %finish.1 = (bf16[192,9216]{1,0:T(8,128)(2,1)}, f32[24,576]{1,0:T(8,128)}, f32[16,1,576]{2,1,0:T(1,128)}) custom-call(bf16[192,9216]{1,0:T(8,128)(2,1)S(1)} %get-tuple-element.7.grad_ref, f32[128,640]{1,0:T(8,128)S(1)} %get-tuple-element.8.rows_ref, f32[24,640]{1,0:T(8,128)S(1)} %get-tuple-element.9.sum_ref, f32[128,128]{1,0:T(8,128)S(1)} %get-tuple-element.10.collect_ref), custom_call_target="tpu_custom_call" | custom-call | tf_op jit(solution)/shard_map/finish/pallas_call | solution.py:466

commit v8 on v7

--- a/solution.py
+++ b/solution.py
@@ -256,11 +256,11 @@
             delta = delta + factor[part] * stats[c, 3 * part + 2:3 * part + 3, :]
         inv = 1.0 / total
         delta = delta * inv
-        for part in range(2):
-            rows = slice(192 * part, 192 * part + 192)
-            pb = eown[c, rows, :] * (factor[part] * inv)
-            prob[c, rows, :] = pb.astype(BF16)
-            ds[c, rows, :] = (pb * (dpown[c, rows, :] - delta)).astype(BF16)
+        stats[c, 6:7, :] = factor[0] * inv
+        stats[c, 7:8, :] = delta
+        pb = eown[c, 192:384, :] * (factor[1] * inv)
+        prob[c, 192:384, :] = pb.astype(BF16)
+        ds[c, 192:384, :] = (pb * (dpown[c, 192:384, :] - delta)).astype(BF16)
         pb = el * inv
         prob[c, 384:448, :] = pb.astype(BF16)
         ds[c, 384:448, :] = (pb * (dpl - delta)).astype(BF16)
@@ -313,8 +313,11 @@
 
     def own_keys(c):
         u, par = chunks[c]
-        dk = dot(ds[c, 0:192, :], q_of(u, par), 1, 0)
-        dv = dot(prob[c, 0:192, :], do_of(u, par), 1, 0)
+        pb = eown[c, 0:192, :] * stats[c, 6:7, :]
+        score = (pb * (dpown[c, 0:192, :] - stats[c, 7:8, :])).astype(BF16)
+        ds[c, 0:192, :] = score
+        dk = dot(score, q_of(u, par), 1, 0)
+        dv = dot(pb.astype(BF16), do_of(u, par), 1, 0)
         if u == 0:
             acc_k[par, 0:192, :] = dk
         else:

time: 46.6 us -> 46.3 us (level)
  no operation moved by 1% of the time
where the time goes in v8:
time: 46.3 us; the launch traced here: 46.2 us
  Pallas kernels  45.6 us (98%)
  between operations  0.64 us (1%)
    pallas_call x1, Pallas kernels, fused_call(): pl.pallas_call(functools.partial(fused, comm), out_shape=(pltpu.VMEM((192...  43.7 us
    pallas_call x1, Pallas kernels, finish_call(): pl.pallas_call(finish, out_shape=(jax.ShapeDtypeStruct((192, 9216), BF16)...  1.83 us

profile of v8, /device:TPU:1, one launch (start us, length us, event | category | flops | bytes accessed | tf_op | source)
XLA Modules:
  0.0 46.2 jit_solution(17604432944836762631)
XLA Ops:
  0.6 43.7 %backward.1 = (bf16[192,9216]{1,0:T(8,128)(2,1)S(1)}, f32[24,640]{1,0:T(8,128)S(1)}, f32[128,640]{1,0:T(8,128)S(1)}, f32[128,128]{1,0:T(8,128)S(1)}) custom-call(s32[32,32]{1,0:T(8,128)} %anc_hbm.1, s32[32]{0:T(128)} %cnt_hbm.1, bf16[192,576]{1,0:T(8,128)(2,1)} %own_hbm.1, bf16[16,8,576]{2,1,0:T(8,128)(2,1)} %trunk_hbm.1, bf16[192,9216]{1,0:T(8,128)(2,1)} %q_hbm.1, ...), custom_call_target="tpu_custom_call" | custom-call | tf_op jit(solution)/shard_map/backward/pallas_call | solution.py:405
  44.4 1.8 %finish.1 = (bf16[192,9216]{1,0:T(8,128)(2,1)}, f32[24,576]{1,0:T(8,128)}, f32[16,1,576]{2,1,0:T(1,128)}) custom-call(bf16[192,9216]{1,0:T(8,128)(2,1)S(1)} %get-tuple-element.7.grad_ref, f32[128,640]{1,0:T(8,128)S(1)} %get-tuple-element.8.rows_ref, f32[24,640]{1,0:T(8,128)S(1)} %get-tuple-element.9.sum_ref, f32[128,128]{1,0:T(8,128)S(1)} %get-tuple-element.10.collect_ref), custom_call_target="tpu_custom_call" | custom-call | tf_op jit(solution)/shard_map/finish/pallas_call | solution.py:469
